TPU v7x, 128 devices: a whole 4x4x4 slice. The times are simulated.
128 devices in a mesh: section: 4 (over x_lo, core), ctx: 8 (over x_hi, z), tp: 4 (over y).
Axes of the slice: x: 4 (x_hi: 2, x_lo: 2; x = x_hi * 2 + x_lo), y: 4, z: 4, core: 2. Of those that a mesh axis runs over, the one named last changes fastest.
Arguments:
- stretch_order: int32 [8, 2], replicated, may hold values from 0 to 15, as said below
- queries: bfloat16 [4, 4096, 2048], P('section', 'ctx', 'tp'), may hold values from -60 to 60
- key_rows: bfloat16 [4, 4096, 512], P('section', 'ctx', 'tp'), may hold values from -7 to 7
- value_rows: bfloat16 [4, 4096, 512], P('section', 'ctx', 'tp'), may hold values from -5 to 5
- out_grad: bfloat16 [4, 4096, 4096], P('section', ('ctx', 'tp')), may hold values from -6 to 6
- query_weight: bfloat16 [4, 4096, 2048], P('section', None, 'tp'), may hold values from -0.09375 to 0.09375
- key_weight: bfloat16 [4, 4096, 512], P('section', None, 'tp'), may hold values from -0.09375 to 0.09375
- value_weight: bfloat16 [4, 4096, 512], P('section', None, 'tp'), may hold values from -0.09375 to 0.09375
- output_weight: bfloat16 [4, 2048, 4096], P('section', 'tp'), may hold values from -0.125 to 0.125
Outputs:
- sent_grad: bfloat16 [4, 4096, 4096], P('section', ('ctx', 'tp'))
- key_grad: bfloat16 [4, 4096, 512], P('section', 'ctx', 'tp')
- value_grad: bfloat16 [4, 4096, 512], P('section', 'ctx', 'tp')
Inputs may be any that keep to these rules, and one draw needn't show every extreme that they name: `stretch_order`: row c lists the ids of the two blocks of 256 consecutive positions stored, in that order, at ctx index c; the two ids of a row sum to 15 and every id occurs once.
All inputs are finite; a program needn't handle non-finite values.
Results may differ from a plain program's by a relative error of at most 0.015.
Values may be sent and summed in bfloat16 or wider, within the bound.
No kernel may reach another device: no remote copies, remote signals or barrier semaphores. Data moves between devices by JAX's collectives and lax.ppermute only.
A program may use at most 128 MiB of HBM per device.

v0:
```python
import jax
import jax.numpy as jnp
from jax import lax
from jax.experimental import pallas as pl
from jax.experimental.pallas import tpu as pltpu
from jax.sharding import PartitionSpec as P

HD = 128
BLK = 256
GROUP = 4
STEPS = 17
SCALE = HD ** (-0.5)
EXP2_SCALE = SCALE * 1.4426950408889634
NEG_LARGE = -1e30

VMEM_WHOLE = pl.BlockSpec(memory_space=pltpu.VMEM)
TP, CTX, SECTION = "tp", "ctx", "section"
PARAMS = pltpu.CompilerParams(vmem_limit_bytes=36 << 20)


def dot_nt(lhs, rhs):
    return lax.dot_general(lhs, rhs, (((1,), (1,)), ((), ())), preferred_element_type=jnp.float32)


def dot_nn(lhs, rhs):
    return lax.dot_general(lhs, rhs, (((1,), (0,)), ((), ())), preferred_element_type=jnp.float32)


def ring(size, shift):
    return [(i, (i + shift) % size) for i in range(size)]


def z_ring(shift):
    return [(x * 4 + z, x * 4 + (z + shift) % 4) for x in range(2) for z in range(4)]


X_SWAP = [(x * 4 + z, (1 - x) * 4 + z) for x in range(2) for z in range(4)]


def joint_ring(shift):
    return [(s * 4 + t, ((s - 1) % 4) * 4 + (t + shift) % 4) for s in range(4) for t in range(4)]


def step_block(step, split):
    half = (step > split).astype(jnp.int32)
    return half, step - half * (split + 1)


def step_args(step, split):
    half, kb = step_block(step, split)
    diag = ((step == split) | (step == STEPS - 1)).astype(jnp.int32)
    return half, kb, diag


def forward_kernel(split_ref, ids_ref, *refs):
    kv_refs = refs[:8]
    (
        q_ref, p_ref, out_ref, stat_ref, hist_ref, kvs_ref,
        max_ref, acc_ref, bias_ref, even_ref, odd_ref, even_top_ref, odd_top_ref,
    ) = refs[8:]
    step = pl.program_id(0)
    split = split_ref[0]
    _, kb, diag = step_args(step, split)

    def score_step(at, score_ref, top_ref):
        at_half, at_kb, at_diag = step_args(at, split)
        start = pl.multiple_of(at_half * BLK, BLK)
        key_blk = kvs_ref[at_kb, :, :HD]
        for h in range(GROUP):
            query = q_ref[pl.ds(start, BLK), h * HD : (h + 1) * HD]
            scores = dot_nt(key_blk, query) + bias_ref[at_diag]
            score_ref[h] = scores
            top_ref[0:1, h * BLK : (h + 1) * BLK] = jnp.max(scores, axis=0, keepdims=True)

    @pl.when(step == 0)
    def _():
        for j in range(8):
            for r in range(2):
                kvs_ref[ids_ref[2 * j + r]] = kv_refs[j][r * BLK : (r + 1) * BLK, :]
        gap = lax.broadcasted_iota(jnp.int32, (BLK, BLK), 0) - lax.broadcasted_iota(
            jnp.int32, (BLK, BLK), 1
        )
        bias_ref[0] = jnp.zeros((BLK, BLK), jnp.float32)
        bias_ref[1] = jnp.where(gap <= 0, 0.0, NEG_LARGE)
        max_ref[...] = jnp.full_like(max_ref, NEG_LARGE)
        acc_ref[...] = jnp.zeros_like(acc_ref)
        score_step(step, even_ref, even_top_ref)

    def softmax_step(now, now_top, later, later_top):
        score_step(jnp.minimum(step + 1, STEPS - 1), later, later_top)
        value_t = jnp.transpose(kvs_ref[kb, :, HD:].astype(jnp.float32)).astype(jnp.bfloat16)
        lhs = jnp.concatenate([value_t, jnp.ones((16, BLK), jnp.bfloat16)], axis=0)
        for h in range(GROUP):
            cols = slice(h * BLK, (h + 1) * BLK)
            old_max = jnp.where(kb == 0, NEG_LARGE, max_ref[0:1, cols])
            new_max = jnp.maximum(old_max, now_top[0:1, cols])
            probs = jnp.exp2((now[h] - new_max) * EXP2_SCALE).astype(jnp.bfloat16)
            p_ref[step, h] = probs
            factor = jnp.exp2((old_max - new_max) * EXP2_SCALE)
            acc_ref[:, cols] = acc_ref[:, cols] * factor + dot_nn(lhs, probs)
            max_ref[0:1, cols] = new_max
            hist_ref[0, 0:1, cols] = new_max

    @pl.when(step % 2 == 0)
    def _():
        softmax_step(even_ref, even_top_ref, odd_ref, odd_top_ref)

    @pl.when(step % 2 == 1)
    def _():
        softmax_step(odd_ref, odd_top_ref, even_ref, even_top_ref)

    @pl.when(diag == 1)
    def _():
        inv = 1.0 / acc_ref[HD : HD + 1, :]
        out_ref[0] = acc_ref[:HD, :] * inv
        stat_ref[0, 0:1, :] = max_ref[0:1, :]
        stat_ref[0, 1:2, :] = inv


def half_of(step, split_ref):
    return (step > split_ref[0]).astype(jnp.int32)


def block_of(step, split_ref):
    return step - half_of(step, split_ref) * (split_ref[0] + 1)


def forward_call(split, ids, kv_chunks, queries):
    whole = pl.BlockSpec((2 * BLK, 2 * HD), lambda i, s, d: (0, 0))
    wide = GROUP * BLK
    return pl.pallas_call(
        forward_kernel,
        grid_spec=pltpu.PrefetchScalarGridSpec(
            num_scalar_prefetch=2,
            grid=(STEPS,),
            in_specs=[whole] * 8 + [pl.BlockSpec((2 * BLK, GROUP * HD), lambda i, s, d: (0, 0))],
            out_specs=[
                VMEM_WHOLE,
                pl.BlockSpec((1, HD, wide), lambda i, s, d: (half_of(i, s), 0, 0)),
                pl.BlockSpec((1, 8, wide), lambda i, s, d: (half_of(i, s), 0, 0)),
                pl.BlockSpec((1, 1, wide), lambda i, s, d: (i, 0, 0)),
                pl.BlockSpec((16, BLK, 2 * HD), lambda i, s, d: (0, 0, 0)),
            ],
            scratch_shapes=[
                pltpu.VMEM((8, wide), jnp.float32),
                pltpu.VMEM((HD + 16, wide), jnp.float32),
                pltpu.VMEM((2, BLK, BLK), jnp.float32),
                pltpu.VMEM((GROUP, BLK, BLK), jnp.float32),
                pltpu.VMEM((GROUP, BLK, BLK), jnp.float32),
                pltpu.VMEM((8, wide), jnp.float32),
                pltpu.VMEM((8, wide), jnp.float32),
            ],
        ),
        out_shape=[
            jax.ShapeDtypeStruct((STEPS, GROUP, BLK, BLK), jnp.bfloat16),
            jax.ShapeDtypeStruct((2, HD, wide), jnp.float32),
            jax.ShapeDtypeStruct((2, 8, wide), jnp.float32),
            jax.ShapeDtypeStruct((STEPS, 1, wide), jnp.float32),
            jax.ShapeDtypeStruct((16, BLK, 2 * HD), jnp.bfloat16),
        ],
        compiler_params=PARAMS,
        cost_estimate=pl.CostEstimate(
            flops=2 * 2 * STEPS * wide * BLK * HD,
            bytes_accessed=13 << 20,
            transcendentals=STEPS * wide * BLK,
        ),
    )(split, ids, *kv_chunks, queries)


def grad_kernel(rows_ref, *refs):
    pieces = refs[:7]
    weight_ref, out_ref, lhs_ref, acc_ref = refs[7:]
    step = pl.program_id(0)
    depth = lhs_ref.shape[1]

    @pl.when(step == 0)
    def _():
        acc_ref[...] = jnp.zeros_like(acc_ref)

    for j, piece in enumerate(pieces):
        size = piece.shape[0]
        lhs_ref[pl.ds(pl.multiple_of(rows_ref[j], 64), size), :] = piece[...]
    start = pl.multiple_of(step * depth, depth)
    acc_ref[...] += dot_nt(lhs_ref[...], weight_ref[:, pl.ds(start, depth)])

    @pl.when(step == pl.num_programs(0) - 1)
    def _():
        out_ref[...] = acc_ref[...].astype(jnp.bfloat16)


def grad_call(rows, pieces, out_weight):
    depth = 1024
    total = out_weight.shape[0]
    return pl.pallas_call(
        grad_kernel,
        grid_spec=pltpu.PrefetchScalarGridSpec(
            num_scalar_prefetch=1,
            grid=(out_weight.shape[1] // depth,),
            in_specs=[pl.BlockSpec((p.shape[0], depth), lambda i, w: (0, i)) for p in pieces]
            + [VMEM_WHOLE],
            out_specs=pl.BlockSpec((2 * BLK, total), lambda i, w: (0, 0)),
            scratch_shapes=[
                pltpu.VMEM((2 * BLK, depth), jnp.bfloat16),
                pltpu.VMEM((2 * BLK, total), jnp.float32),
            ],
        ),
        out_shape=jax.ShapeDtypeStruct((2 * BLK, total), jnp.bfloat16),
        compiler_params=PARAMS,
        cost_estimate=pl.CostEstimate(
            flops=2 * 2 * BLK * total * out_weight.shape[1],
            bytes_accessed=9 << 20,
            transcendentals=0,
        ),
    )(rows, *pieces, out_weight)


def norm_of(hist_ref, stat_ref, cols):
    gap = (hist_ref[0, 0:1, cols] - stat_ref[0, 0:1, cols]) * EXP2_SCALE
    return jnp.exp2(gap) * stat_ref[0, 1:2, cols]


def group_rows(ids_ref, chunk_ref, total_ref, group, x, index):
    chunk = chunk_ref[index]
    block = ids_ref[4 * group + 2 * x + chunk // 2]
    start = pl.multiple_of((chunk % 2) * 128, 128)
    return total_ref[block, pl.ds(start, 128), :]


def value_kernel(split_ref, ids_ref, chunk_ref, grad_ref, p_ref, stat_ref, hist_ref, *refs):
    group_refs = refs[:4]
    total_ref = refs[4]
    step = pl.program_id(0)
    half, kb, _ = step_args(step, split_ref[0])

    @pl.when(step == 0)
    def _():
        total_ref[...] = jnp.zeros_like(total_ref)

    start = pl.multiple_of(half * BLK, BLK)
    dv = jnp.zeros((BLK, HD), jnp.float32)
    for h in range(GROUP):
        norm = norm_of(hist_ref, stat_ref, slice(h * BLK, (h + 1) * BLK))
        probs = (p_ref[step, h].astype(jnp.float32) * norm).astype(jnp.bfloat16)
        dv = dv + dot_nn(probs, grad_ref[pl.ds(start, BLK), h * HD : (h + 1) * HD])
    total_ref[kb] += dv

    @pl.when(step == STEPS - 1)
    def _():
        for g, g_ref in enumerate(group_refs):
            for x in range(2):
                for j in range(4):
                    rows = group_rows(ids_ref, chunk_ref, total_ref, g, x, j)
                    g_ref[x, j * 128 : (j + 1) * 128, :] = rows.astype(jnp.bfloat16)


def value_call(split, ids, chunks, grad, saved):
    probs, _, stats, hist, _ = saved
    wide = GROUP * BLK
    group_spec = pl.BlockSpec((2, 2 * BLK, HD), lambda i, s, d, c: (0, 0, 0))
    return pl.pallas_call(
        value_kernel,
        grid_spec=pltpu.PrefetchScalarGridSpec(
            num_scalar_prefetch=3,
            grid=(STEPS,),
            in_specs=[
                pl.BlockSpec((2 * BLK, GROUP * HD), lambda i, s, d, c: (0, 0)),
                VMEM_WHOLE,
                pl.BlockSpec((1, 8, wide), lambda i, s, d, c: (half_of(i, s), 0, 0)),
                pl.BlockSpec((1, 1, wide), lambda i, s, d, c: (i, 0, 0)),
            ],
            out_specs=[group_spec] * 4,
            scratch_shapes=[pltpu.VMEM((16, BLK, HD), jnp.float32)],
        ),
        out_shape=[jax.ShapeDtypeStruct((2, 2 * BLK, HD), jnp.bfloat16)] * 4,
        compiler_params=PARAMS,
        cost_estimate=pl.CostEstimate(
            flops=2 * STEPS * wide * BLK * HD, bytes_accessed=11 << 20, transcendentals=0
        ),
        name="attn_value_grad",
    )(split, ids, chunks, grad, probs, stats, hist)


def key_kernel(split_ref, ids_ref, chunk_ref, grad_ref, q_ref, p_ref, kv_ref, next_ref, out_ref, stat_ref,
               hist_ref, *refs):
    dq_ref = refs[0]
    far_refs, rest_refs = refs[1:5], refs[5:9]
    delta_ref, dqt_ref, total_ref, even_ref, odd_ref = refs[9:]
    step = pl.program_id(0)
    split = split_ref[0]
    half, kb, diag = step_args(step, split)

    def grad_probs_step(at, value_blk, gp_ref):
        at_half = (at > split).astype(jnp.int32)
        start = pl.multiple_of(at_half * BLK, BLK)
        for h in range(GROUP):
            gp_ref[h] = dot_nt(
                value_blk, grad_ref[pl.ds(start, BLK), h * HD : (h + 1) * HD]
            )

    @pl.when(step == 0)
    def _():
        total_ref[...] = jnp.zeros_like(total_ref)
        dqt_ref[...] = jnp.zeros_like(dqt_ref)
        grad_probs_step(step, kv_ref[0, :, HD:], even_ref)

    start = pl.multiple_of(half * BLK, BLK)

    @pl.when(kb == 0)
    def _():
        for h in range(GROUP):
            cols = slice(h * BLK, (h + 1) * BLK)
            grad = grad_ref[pl.ds(start, BLK), h * HD : (h + 1) * HD]
            grad_t = jnp.transpose(grad.astype(jnp.float32))
            delta_ref[0:1, cols] = jnp.sum(out_ref[0, :, cols] * grad_t, axis=0, keepdims=True)

    def main_step(now, later):
        grad_probs_step(jnp.minimum(step + 1, STEPS - 1), next_ref[0, :, HD:], later)
        key_t = jnp.transpose(kv_ref[0, :, :HD].astype(jnp.float32)).astype(jnp.bfloat16)
        keep = jnp.where(kb == 0, 0.0, 1.0)
        dk = jnp.zeros((BLK, HD), jnp.float32)
        for h in range(GROUP):
            cols = slice(h * BLK, (h + 1) * BLK)
            probs = p_ref[step, h].astype(jnp.float32) * norm_of(hist_ref, stat_ref, cols)
            dscore = (probs * (now[h] - delta_ref[0:1, cols])).astype(jnp.bfloat16)
            dk = dk + dot_nn(dscore, q_ref[pl.ds(start, BLK), h * HD : (h + 1) * HD])
            dqt_ref[:, cols] = dqt_ref[:, cols] * keep + dot_nn(key_t, dscore)
        total_ref[kb] += dk

    @pl.when(step % 2 == 0)
    def _():
        main_step(even_ref, odd_ref)

    @pl.when(step % 2 == 1)
    def _():
        main_step(odd_ref, even_ref)

    @pl.when(diag == 1)
    def _():
        for h in range(GROUP):
            cols = slice(h * BLK, (h + 1) * BLK)
            dq_ref[:, h * HD : (h + 1) * HD] = jnp.transpose(dqt_ref[:, cols] * SCALE).astype(
                jnp.bfloat16
            )

    @pl.when(step == STEPS - 1)
    def _():
        for g in range(4):
            for x in range(2):
                for j in range(4):
                    rows = group_rows(ids_ref, chunk_ref, total_ref, g, x, j)
                    rows = (rows * SCALE).astype(jnp.bfloat16)
                    if j == 0:
                        far_refs[g][x] = rows
                    else:
                        rest_refs[g][x, (j - 1) * 128 : j * 128, :] = rows


def key_call(split, ids, chunks, grad, saved, queries):
    probs, outs, stats, hist, kv_sorted = saved
    wide = GROUP * BLK
    shapes = [(2, 128, HD)] * 4 + [(2, 2 * BLK - 128, HD)] * 4
    whole = pl.BlockSpec((2 * BLK, GROUP * HD), lambda i, s, d, c: (0, 0))

    def next_block(i, s, d, c):
        return (block_of(jnp.minimum(i + 1, STEPS - 1), s), 0, 0)

    return pl.pallas_call(
        key_kernel,
        grid_spec=pltpu.PrefetchScalarGridSpec(
            num_scalar_prefetch=3,
            grid=(STEPS,),
            in_specs=[
                whole,
                whole,
                VMEM_WHOLE,
                pl.BlockSpec((1, BLK, 2 * HD), lambda i, s, d, c: (block_of(i, s), 0, 0)),
                pl.BlockSpec((1, BLK, 2 * HD), next_block),
                pl.BlockSpec((1, HD, wide), lambda i, s, d, c: (half_of(i, s), 0, 0)),
                pl.BlockSpec((1, 8, wide), lambda i, s, d, c: (half_of(i, s), 0, 0)),
                pl.BlockSpec((1, 1, wide), lambda i, s, d, c: (i, 0, 0)),
            ],
            out_specs=[pl.BlockSpec((BLK, GROUP * HD), lambda i, s, d, c: (half_of(i, s), 0))]
            + [pl.BlockSpec(shape, lambda i, s, d, c: (0, 0, 0)) for shape in shapes],
            scratch_shapes=[
                pltpu.VMEM((8, wide), jnp.float32),
                pltpu.VMEM((HD, wide), jnp.float32),
                pltpu.VMEM((16, BLK, HD), jnp.float32),
                pltpu.VMEM((GROUP, BLK, BLK), jnp.float32),
                pltpu.VMEM((GROUP, BLK, BLK), jnp.float32),
            ],
        ),
        out_shape=[jax.ShapeDtypeStruct((2 * BLK, GROUP * HD), jnp.bfloat16)]
        + [jax.ShapeDtypeStruct(shape, jnp.bfloat16) for shape in shapes],
        compiler_params=PARAMS,
        cost_estimate=pl.CostEstimate(
            flops=2 * 3 * STEPS * wide * BLK * HD, bytes_accessed=14 << 20, transcendentals=0
        ),
    )(split, ids, chunks, grad, queries, probs, kv_sorted, kv_sorted, outs, stats, hist)


def per_device(
    stretch_order,
    queries,
    key_rows,
    value_rows,
    out_grad,
    query_weight,
    key_weight,
    value_weight,
    output_weight,
):
    send = lax.ppermute
    tp = lax.axis_index(TP)
    ctx = lax.axis_index(CTX)
    own_x, own_z = ctx // 4, ctx % 4
    bf16 = jnp.bfloat16

    chunk = out_grad[0]
    half_rows = chunk.shape[0] // 2
    top, low = chunk[:half_rows], chunk[half_rows:]
    left_top = send(top, TP, ring(4, 1))
    right_low = send(low, TP, ring(4, -1))
    far_top = send(left_top, TP, ring(4, 1))
    far_low = send(right_low, TP, ring(4, -1))
    left_low = send(low, TP, ring(4, 1))
    right_top = send(top, TP, ring(4, -1))

    kv_own = jnp.concatenate([key_rows[0], value_rows[0]], axis=1)
    kv_pair = send(kv_own, CTX, X_SWAP)
    along, crossed = {}, {}
    for distance, shift in ((2, 2), (1, -1), (3, 1)):
        along[distance] = send(kv_own, CTX, z_ring(shift))
    for distance, shift in ((1, -1), (3, 1)):
        crossed[distance] = send(kv_pair, CTX, z_ring(shift))
    crossed[2] = send(along[2], CTX, X_SWAP)
    kv_chunks = [kv_own, kv_pair]
    for distance in (1, 2, 3):
        kv_chunks += [along[distance], crossed[distance]]

    kv_weights = jnp.concatenate([key_weight[0], value_weight[0]], axis=1)
    kv_weights = lax.optimization_barrier(kv_weights)
    sent_weights = send(kv_weights, SECTION, ring(4, -1))

    index = jnp.arange(8, dtype=jnp.int32)
    source = ((own_x + index % 2) % 2) * 4 + (own_z + index // 2) % 4
    table = jnp.arange(8, dtype=jnp.int32)
    ids = jnp.sum(
        jnp.where(source[:, None, None] == table[None, :, None], stretch_order[None], 0), axis=1
    ).reshape(16)
    split = ids[:1]
    saved = forward_call(split, ids, kv_chunks, queries[0])

    left, right, far = (tp + 3) % 4, (tp + 1) % 4, (tp + 2) % 4
    pieces = (chunk, left_top, left_low, right_top, right_low, far_top, far_low)
    places = (2 * tp, 2 * left, 2 * left + 1, 2 * right, 2 * right + 1, 2 * far, 2 * far + 1)
    grad = grad_call(
        (jnp.stack(places) * half_rows).astype(jnp.int32), pieces, output_weight[0]
    )

    f32 = jnp.float32

    def along_z(groups):
        total = groups[0].astype(f32)
        for distance, shift in ((1, 1), (2, 2), (3, -1)):
            received = send(groups[distance], CTX, z_ring(shift))
            total = total + received.astype(f32)
        return total

    chunks = jnp.stack([far, left, tp, right]).astype(jnp.int32)
    groups, grad = lax.optimization_barrier((value_call(split, ids, chunks, grad, saved), grad))
    value_sum = along_z(groups)
    query_grad, *groups = key_call(split, ids, chunks, grad, saved, queries[0])
    *near_weights, query_grad = lax.optimization_barrier(
        (key_weight[0], value_weight[0], query_grad)
    )
    near_weights = jnp.concatenate(near_weights, axis=1)
    key_far_sum = along_z(groups[:4])
    key_rest_sum = along_z(groups[4:])

    def with_pair(total):
        received = send(total[1].astype(bf16), CTX, X_SWAP)
        return (total[0] + received.astype(f32)).astype(bf16)

    def chunk_of(array, distance):
        return lax.dynamic_slice_in_dim(array, ((tp + distance) % 4) * 128, 128, 0)

    query_terms = []
    for distance in range(4):
        query_terms.append(dot_nt(chunk_of(query_grad, distance), query_weight[0]))
    query_terms[0] = query_terms[0].astype(bf16)
    query_terms = [lax.optimization_barrier(term) for term in query_terms]
    own = send(query_terms[0], SECTION, ring(4, -1))

    value_grad = with_pair(value_sum)
    key_far = with_pair(key_far_sum)
    key_rest = with_pair(key_rest_sum)

    def rows_of(distance):
        j = (distance + 2) % 4
        key_rows = key_far if j == 0 else key_rest[(j - 1) * 128 : j * 128]
        return jnp.concatenate([key_rows, value_grad[j * 128 : (j + 1) * 128]], axis=1)

    def in_order(array):
        return lax.dynamic_slice_in_dim(
            jnp.concatenate([array, array], axis=0), ((2 - tp) % 4) * 128, array.shape[0], 0
        )

    def term_of(distance):
        return (query_terms[distance] + dot_nt(rows_of(distance), near_weights)).astype(bf16)

    far = term_of(2)
    from_left = send(far[:half_rows], TP, ring(4, 1))
    from_right = send(far[half_rows:], TP, ring(4, -1))
    right, left = lax.optimization_barrier((term_of(1), term_of(3)))
    joint = (SECTION, TP)
    low_a = send(right[half_rows:], joint, joint_ring(1))
    top_b = send(left[:half_rows], joint, joint_ring(-1))
    rows = send(rows_of(0), SECTION, ring(4, -1))
    own = lax.optimization_barrier(own.astype(f32) + dot_nt(rows, sent_weights))
    top_a = (right[:half_rows].astype(f32) + from_left.astype(f32)).astype(bf16)
    top_a = send(top_a, joint, joint_ring(1))
    low_b = (left[half_rows:].astype(f32) + from_right.astype(f32)).astype(bf16)
    low_b = send(low_b, joint, joint_ring(-1))
    sent = jnp.concatenate(
        [
            own[:half_rows] + top_a.astype(f32) + top_b.astype(f32),
            own[half_rows:] + low_a.astype(f32) + low_b.astype(f32),
        ],
        axis=0,
    ).astype(bf16)
    key_grad = in_order(jnp.concatenate([key_far, key_rest], axis=0))
    return (sent[None], key_grad[None], in_order(value_grad)[None])


def solution(mesh):
    placed = (
        P(),
        P(SECTION, CTX, TP),
        P(SECTION, CTX, TP),
        P(SECTION, CTX, TP),
        P(SECTION, (CTX, TP), None),
        P(SECTION, None, TP),
        P(SECTION, None, TP),
        P(SECTION, None, TP),
        P(SECTION, TP, None),
    )

    return jax.shard_map(
        per_device,
        mesh=mesh,
        in_specs=placed,
        out_specs=(
            P(SECTION, (CTX, TP), None),
            P(SECTION, CTX, TP),
            P(SECTION, CTX, TP),
        ),
        check_vma=False,
    )
```

profile of v0, /device:TPU:1, one launch (start us, length us, event | category | flops | bytes accessed | tf_op | source)
XLA Modules:
  0.0 179.8 jit_solution(12335984365760927245)
XLA Ops:
  1.8 3.6 %collective-permute-start.6 = (bf16[512,256]{1,0:T(8,128)(2,1)S(1)}, bf16[512,256]{1,0:T(8,128)(2,1)}, u32[]{:S(2)}, u32[]{:S(2)}) collective-permute-start(bf16[512,256]{1,0:T(8,128)(2,1)S(1)} %pad_maximum_fusion.2.refs_0_), channel_id=1, source_target_pairs={{0,16},{4,20},{8,24},{12,28},{16,0},{20,4},{24,8},{28,12},{1,17},{... | collective-permute-start | bytes 786440 | tf_op jit(solution)/shard_map/ppermute | solution.py:429
  5.4 3.8 %collective-permute-start.7 = (bf16[512,256]{1,0:T(8,128)(2,1)S(1)}, bf16[512,256]{1,0:T(8,128)(2,1)S(1)}, u32[]{:S(2)}, u32[]{:S(2)}) collective-permute-start(bf16[512,256]{1,0:T(8,128)(2,1)S(1)} %pad_maximum_fusion.2.refs_0_), channel_id=1, source_target_pairs={{0,12},{4,0},{8,4},{12,8},{16,28},{20,16},{24,20},{28,24},{1,13},{... | collective-permute-start | bytes 786440 | tf_op jit(solution)/shard_map/ppermute | solution.py:432
  9.2 2.3 %slice_bitcast_fusion = (bf16[64,4096]{1,0:T(8,128)(2,1)}, bf16[64,4096]{1,0:T(8,128)(2,1)}) fusion(bf16[1,128,4096]{2,1,0:T(8,128)(2,1)} %param.13), kind=kLoop, calls=%fused_computation.28 | loop fusion | bytes 2097152 | tf_op jit(solution)/shard_map/slice | solution.py:420
  14.2 1.6 pad_maximum_fusion
  16.6 2.8 %collective-permute-done.7.refs_2_ = bf16[512,256]{1,0:T(8,128)(2,1)S(1)} collective-permute-done((bf16[512,256]{1,0:T(8,128)(2,1)S(1)}, bf16[512,256]{1,0:T(8,128)(2,1)S(1)}, u32[]{:S(2)}, u32[]{:S(2)}) %collective-permute-start.7) | collective-permute-done | bytes 262176 | tf_op jit(solution)/shard_map/ppermute | solution.py:432
  20.1 3.6 %collective-permute-start.8 = (bf16[512,256]{1,0:T(8,128)(2,1)}, bf16[512,256]{1,0:T(8,128)(2,1)S(1)}, u32[]{:S(2)}, u32[]{:S(2)}) collective-permute-start(bf16[512,256]{1,0:T(8,128)(2,1)} %collective-permute-done.6.refs_1_), channel_id=1, source_target_pairs={{0,12},{4,0},{8,4},{12,8},{16,28},{20,16},{24,20},{28,24},{1,13},{... | collective-permute-start | bytes 786440 | tf_op jit(solution)/shard_map/ppermute | solution.py:434
  26.8 1.4 collective-permute-start.2
  31.6 2.7 %collective-permute-start.5 = (bf16[64,4096]{1,0:T(8,128)(2,1)S(1)}, bf16[64,4096]{1,0:T(8,128)(2,1)S(1)}, u32[]{:S(2)}, u32[]{:S(2)}) collective-permute-start(bf16[64,4096]{1,0:T(8,128)(2,1)S(1)} %collective-permute-done.3.refs_4_), channel_id=1, source_target_pairs={{0,3},{1,0},{2,1},{3,2},{4,7},{5,4},{6,5},{7,6},{8,11},{9,8},{10,9... | collective-permute-start | bytes 1572872 | tf_op jit(solution)/shard_map/ppermute | solution.py:424
  35.2 3.8 %collective-permute-start.23 = (bf16[4096,256]{1,0:T(8,128)(2,1)}, bf16[4096,256]{1,0:T(8,128)(2,1)}, u32[]{:S(2)}, u32[]{:S(2)}) collective-permute-start(bf16[4096,256]{1,0:T(8,128)(2,1)} %pad_maximum_fusion), channel_id=1, source_target_pairs={{0,96},{32,0},{64,32},{96,64},{1,97},{33,1},{65,33},{97,65},{2,98}... | collective-permute-start | bytes 6291464 | tf_op jit(solution)/shard_map/ppermute | solution.py:442
  44.8 10.9 %shard_map.113 = (bf16[17,4,256,256]{3,2,1,0:T(8,128)(2,1)S(1)}, f32[2,128,1024]{2,1,0:T(8,128)S(1)}, f32[2,8,1024]{2,1,0:T(8,128)S(1)}, f32[17,1,1024]{2,1,0:T(1,128)S(1)}, bf16[16,256,256]{2,1,0:T(8,128)(2,1)S(1)}) custom-call(s32[1]{0:T(128)S(1)} %bitcast.73, s32[16]{0:T(128)S(1)} %reshape.116.ids_ref, bf16[512,256]{1,0:T(8,128)(2,1)S(1)} %pad_maximum_fusion.2.refs_0_, ...), custom_call_target="tpu_custom_call" | custom-call | flops 2281701376 | bytes 13631488 | tf_op jit(solution)/shard_map/pallas_call | solution.py:131
  55.8 4.2 %shard_map.112.grad_ref = bf16[512,512]{1,0:T(8,128)(2,1)S(1)} custom-call(s32[7]{0:T(128)S(1)} %broadcast_multiply_fusion.rows_ref, bf16[128,4096]{1,0:T(8,128)(2,1)S(1)} %bitcast.69, bf16[64,4096]{1,0:T(8,128)(2,1)S(1)} %collective-permute-done.refs_1_, bf16[64,4096]{1,0:T(8,128)(2,1)S(1)} %collective-permute-done.1.refs_2_, ...), custom_call_target="tpu_custom_call" | custom-call | flops 2147483648 | bytes 9437184 | tf_op jit(solution)/shard_map/pallas_call | solution.py:194
  60.0 6.2 %attn_value_grad.1 = (bf16[2,512,128]{2,1,0:T(8,128)(2,1)S(1)}, bf16[2,512,128]{2,1,0:T(8,128)(2,1)S(1)}, bf16[2,512,128]{2,1,0:T(8,128)(2,1)S(1)}, bf16[2,512,128]{2,1,0:T(8,128)(2,1)S(1)}) custom-call(s32[1]{0:T(128)S(1)} %bitcast.74, s32[16]{0:T(128)S(1)} %reshape.116.ids_ref, s32[4]{0:T(128)S(1)} %pad_add_fusion.chunk_ref, ...), custom_call_target="tpu_custom_call" | custom-call | flops 1140850688 | bytes 11534336 | tf_op jit(solution)/shard_map/attn_value_grad/pallas_call | solution.py:260
  66.2 12.1 %shard_map.114 = (bf16[512,512]{1,0:T(8,128)(2,1)S(1)}, bf16[2,128,128]{2,1,0:T(8,128)(2,1)S(1)}, bf16[2,128,128]{2,1,0:T(8,128)(2,1)S(1)}, bf16[2,128,128]{2,1,...) custom-call(s32[1]{0:T(128)S(1)} %bitcast.75, ...), custom_call_target="tpu_custom_call" | custom-call | flops 3422552064 | bytes 14680064 | tf_op jit(solution)/shard_map/pallas_call | solution.py:367
  78.5 1.5 fusion.7
  80.0 1.5 fusion.3
  83.9 1.5 convolution_convert_fusion
  85.4 2.2 %collective-permute-start.20 = (bf16[2,512,128]{2,1,0:T(8,128)(2,1)S(1)}, bf16[2,512,128]{2,1,0:T(8,128)(2,1)S(1)}, u32[]{:S(2)}, u32[]{:S(2)}) collective-permute-start(bf16[2,512,128]{2,1,0:T(8,128)(2,1)S(1)} %get-tuple-element.50), channel_id=1, source_target_pairs={{0,12},{4,0},{8,4},{12,8},{16,28},{20,16},{24,20},{28,24},{1,13},{... | collective-permute-start | bytes 786440 | tf_op jit(solution)/shard_map/ppermute | solution.py:465
  88.8 2.8 %collective-permute-start.27 = (bf16[128,128]{1,0:T(8,128)(2,1)S(1)}, bf16[128,128]{1,0:T(8,128)(2,1)S(1)}, u32[]{:S(2)}, u32[]{:S(2)}) collective-permute-start(bf16[128,128]{1,0:T(8,128)(2,1)S(1)} %fusion.43), channel_id=1, source_target_pairs={{0,16},{4,20},{8,24},{12,28},{16,0},{20,4},{24,8},{28,12},{1,17},{... | collective-permute-start | bytes 98312 | tf_op jit(solution)/shard_map/ppermute | solution.py:481
  91.6 1.5 fusion.5
  94.0 3.0 %collective-permute-done.16 = bf16[2,384,128]{2,1,0:T(8,128)(2,1)S(1)} collective-permute-done((bf16[2,384,128]{2,1,0:T(8,128)(2,1)S(1)}, bf16[2,384,128]{2,1,0:T(8,128)(2,1)S(1)}, u32[]{:S(2)}, u32[]{:S(2)}) %collective-permute-start.16) | collective-permute-done | bytes 196640 | tf_op jit(solution)/shard_map/ppermute | solution.py:465
  97.0 2.6 %collective-permute-start.19 = (bf16[2,512,128]{2,1,0:T(8,128)(2,1)S(1)}, bf16[2,512,128]{2,1,0:T(8,128)(2,1)S(1)}, u32[]{:S(2)}, u32[]{:S(2)}) collective-permute-start(bf16[2,512,128]{2,1,0:T(8,128)(2,1)S(1)} %get-tuple-element.49), channel_id=1, source_target_pairs={{0,8},{4,12},{8,0},{12,4},{16,24},{20,28},{24,16},{28,20},{1,9},{5... | collective-permute-start | bytes 786440 | tf_op jit(solution)/shard_map/ppermute | solution.py:465
  99.6 3.6 %collective-permute-start.18 = (bf16[2,512,128]{2,1,0:T(8,128)(2,1)S(1)}, bf16[2,512,128]{2,1,0:T(8,128)(2,1)S(1)}, u32[]{:S(2)}, u32[]{:S(2)}) collective-permute-start(bf16[2,512,128]{2,1,0:T(8,128)(2,1)S(1)} %get-tuple-element.48), channel_id=1, source_target_pairs={{0,4},{4,8},{8,12},{12,0},{16,20},{20,24},{24,28},{28,16},{1,5},{5... | collective-permute-start | bytes 786440 | tf_op jit(solution)/shard_map/ppermute | solution.py:465
  103.2 6.7 %collective-permute-start.13 = (bf16[128,4096]{1,0:T(8,128)(2,1)S(1)}, bf16[128,4096]{1,0:T(8,128)(2,1)S(1)}, u32[]{:S(2)}, u32[]{:S(2)}) collective-permute-start(bf16[128,4096]{1,0:T(8,128)(2,1)S(1)} %convolution_convert_fusion), channel_id=1, source_target_pairs={{0,96},{32,0},{64,32},{96,64},{1,97},{33,1},{65,33},{97,65},{2,98}... | collective-permute-start | bytes 3145736 | tf_op jit(solution)/shard_map/ppermute | solution.py:492
  110.3 5.7 %collective-permute-start.21 = (bf16[512,128]{1,0:T(8,128)(2,1)S(1)}, bf16[512,128]{1,0:T(8,128)(2,1)S(1)}, u32[]{:S(2)}, u32[]{:S(2)}) collective-permute-start(bf16[512,128]{1,0:T(8,128)(2,1)S(1)} %fusion.26), channel_id=1, source_target_pairs={{0,16},{4,20},{8,24},{12,28},{16,0},{20,4},{24,8},{28,12},{1,17},{... | collective-permute-start | bytes 393224 | tf_op jit(solution)/shard_map/ppermute | solution.py:481
  116.2 3.6 %collective-permute-done.21 = bf16[512,128]{1,0:T(8,128)(2,1)S(1)} collective-permute-done((bf16[512,128]{1,0:T(8,128)(2,1)S(1)}, bf16[512,128]{1,0:T(8,128)(2,1)S(1)}, u32[]{:S(2)}, u32[]{:S(2)}) %collective-permute-start.21) | collective-permute-done | bytes 131104 | tf_op jit(solution)/shard_map/ppermute | solution.py:481
  122.9 10.3 %collective-permute-start.30 = (bf16[64,4096]{1,0:T(8,128)(2,1)S(1)}, bf16[64,4096]{1,0:T(8,128)(2,1)S(1)}, u32[]{:S(2)}, u32[]{:S(2)}) collective-permute-start(bf16[64,4096]{1,0:T(8,128)(2,1)S(1)} %slice.102), channel_id=1, source_target_pairs={{0,99},{1,96},{2,97},{3,98},{32,3},{33,0},{34,1},{35,2},{64,35},{6... | collective-permute-start | bytes 1572872 | tf_op jit(solution)/shard_map/ppermute | solution.py:517
  133.8 21.6 %collective-permute-done.32 = bf16[64,4096]{1,0:T(8,128)(2,1)S(1)} collective-permute-done((bf16[64,4096]{1,0:T(8,128)(2,1)S(1)}, bf16[64,4096]{1,0:T(8,128)(2,1)S(1)}, u32[]{:S(2)}, u32[]{:S(2)}) %collective-permute-start.32) | collective-permute-done | bytes 524320 | tf_op jit(solution)/shard_map/ppermute | solution.py:513
  155.6 2.7 %collective-permute-start.29 = (bf16[64,4096]{1,0:T(8,128)(2,1)S(1)}, bf16[64,4096]{1,0:T(8,128)(2,1)S(1)}, u32[]{:S(2)}, u32[]{:S(2)}) collective-permute-start(bf16[64,4096]{1,0:T(8,128)(2,1)S(1)} %add_convert_fusion.1), channel_id=1, source_target_pairs={{0,97},{1,98},{2,99},{3,96},{32,1},{33,2},{34,3},{35,0},{64,33},{6... | collective-permute-start | bytes 1572872 | tf_op jit(solution)/shard_map/ppermute | solution.py:521
  158.7 1.4 fusion.25
  161.3 2.4 %convert_add_fusion = f32[128,4096]{1,0:T(8,128)S(1)} fusion(bf16[128,4096]{1,0:T(8,128)(2,1)S(1)} %collective-permute-done.13, bf16[128,256]{1,0:T(8,128)(2,1)S(1)} %collective-permute-done.22, bf16[4096,256]{1,0:T(8,128)(2,1)} %collective-permute-done.23), kind=kOutput, calls=%fused_computation.15 | convolution fusion | flops 269484032 | bytes 5308416 | tf_op jit(solution)/shard_map/dot_general | solution.py:22
  163.7 9.1 %collective-permute-done.31 = bf16[64,4096]{1,0:T(8,128)(2,1)S(1)} collective-permute-done((bf16[64,4096]{1,0:T(8,128)(2,1)S(1)}, bf16[64,4096]{1,0:T(8,128)(2,1)S(1)}, u32[]{:S(2)}, u32[]{:S(2)}) %collective-permute-start.31) | collective-permute-done | bytes 524320 | tf_op jit(solution)/shard_map/ppermute | solution.py:516
  172.8 5.6 %collective-permute-done.29 = bf16[64,4096]{1,0:T(8,128)(2,1)S(1)} collective-permute-done((bf16[64,4096]{1,0:T(8,128)(2,1)S(1)}, bf16[64,4096]{1,0:T(8,128)(2,1)S(1)}, u32[]{:S(2)}, u32[]{:S(2)}) %collective-permute-start.29) | collective-permute-done | bytes 524320 | tf_op jit(solution)/shard_map/ppermute | solution.py:521
  (122 shorter events, 30.6 us)
Async XLA Ops:
  1.8 14.0 %collective-permute-start.6 = (bf16[512,256]{1,0:T(8,128)(2,1)S(1)}, bf16[512,256]{1,0:T(8,128)(2,1)}, u32[]{:S(2)}, u32[]{:S(2)}) collective-permute-start(bf16[512,256]{1,0:T(8,128)(2,1)S(1)} %pad_maximum_fusion.2.refs_0_), channel_id=1, source_target_pairs={{0,16},{4,20},{8,24},{12,28},{16,0},{20,4},{24,8},{28,12},{1,17},{... | collective-permute-start | bytes 786440 | tf_op jit(solution)/shard_map/ppermute | solution.py:429
  5.4 13.9 %collective-permute-start.7 = (bf16[512,256]{1,0:T(8,128)(2,1)S(1)}, bf16[512,256]{1,0:T(8,128)(2,1)S(1)}, u32[]{:S(2)}, u32[]{:S(2)}) collective-permute-start(bf16[512,256]{1,0:T(8,128)(2,1)S(1)} %pad_maximum_fusion.2.refs_0_), channel_id=1, source_target_pairs={{0,12},{4,0},{8,4},{12,8},{16,28},{20,16},{24,20},{28,24},{1,13},{... | collective-permute-start | bytes 786440 | tf_op jit(solution)/shard_map/ppermute | solution.py:432
  9.2 14.4 %collective-permute-start.9 = (bf16[512,256]{1,0:T(8,128)(2,1)S(1)}, bf16[512,256]{1,0:T(8,128)(2,1)S(1)}, u32[]{:S(2)}, u32[]{:S(2)}) collective-permute-start(bf16[512,256]{1,0:T(8,128)(2,1)S(1)} %pad_maximum_fusion.2.refs_0_), channel_id=1, source_target_pairs={{0,8},{4,12},{8,0},{12,4},{16,24},{20,28},{24,16},{28,20},{1,9},{5... | collective-permute-start | bytes 786440 | tf_op jit(solution)/shard_map/ppermute | solution.py:432
  11.5 15.3 %collective-permute-start = (bf16[64,4096]{1,0:T(8,128)(2,1)}, bf16[64,4096]{1,0:T(8,128)(2,1)S(1)}, u32[]{:S(2)}, u32[]{:S(2)}) collective-permute-start(bf16[64,4096]{1,0:T(8,128)(2,1)} %get-tuple-element.64), channel_id=1, source_target_pairs={{0,1},{1,2},{2,3},{3,0},{4,5},{5,6},{6,7},{7,4},{8,9},{9,10},{10,1... | collective-permute-start | bytes 1572872 | tf_op jit(solution)/shard_map/ppermute | solution.py:421
  12.8 15.5 %collective-permute-start.3 = (bf16[64,4096]{1,0:T(8,128)(2,1)}, bf16[64,4096]{1,0:T(8,128)(2,1)S(1)}, u32[]{:S(2)}, u32[]{:S(2)}) collective-permute-start(bf16[64,4096]{1,0:T(8,128)(2,1)} %get-tuple-element.63), channel_id=1, source_target_pairs={{0,3},{1,0},{2,1},{3,2},{4,7},{5,4},{6,5},{7,6},{8,11},{9,8},{10,9... | collective-permute-start | bytes 1572872 | tf_op jit(solution)/shard_map/ppermute | solution.py:422
  15.8 9.0 %collective-permute-start.11 = (bf16[512,256]{1,0:T(8,128)(2,1)S(1)}, bf16[512,256]{1,0:T(8,128)(2,1)S(1)}, u32[]{:S(2)}, u32[]{:S(2)}) collective-permute-start(bf16[512,256]{1,0:T(8,128)(2,1)S(1)} %pad_maximum_fusion.2.refs_0_), channel_id=1, source_target_pairs={{0,4},{4,8},{8,12},{12,0},{16,20},{20,24},{24,28},{28,16},{1,5},{5... | collective-permute-start | bytes 786440 | tf_op jit(solution)/shard_map/ppermute | solution.py:432
  20.1 8.2 %collective-permute-start.8 = (bf16[512,256]{1,0:T(8,128)(2,1)}, bf16[512,256]{1,0:T(8,128)(2,1)S(1)}, u32[]{:S(2)}, u32[]{:S(2)}) collective-permute-start(bf16[512,256]{1,0:T(8,128)(2,1)} %collective-permute-done.6.refs_1_), channel_id=1, source_target_pairs={{0,12},{4,0},{8,4},{12,8},{16,28},{20,16},{24,20},{28,24},{1,13},{... | collective-permute-start | bytes 786440 | tf_op jit(solution)/shard_map/ppermute | solution.py:434
  23.6 7.3 %collective-permute-start.10 = (bf16[512,256]{1,0:T(8,128)(2,1)S(1)}, bf16[512,256]{1,0:T(8,128)(2,1)S(1)}, u32[]{:S(2)}, u32[]{:S(2)}) collective-permute-start(bf16[512,256]{1,0:T(8,128)(2,1)S(1)} %collective-permute-done.9.refs_4_), channel_id=1, source_target_pairs={{0,16},{4,20},{8,24},{12,28},{16,0},{20,4},{24,8},{28,12},{1,17},{... | collective-permute-start | bytes 786440 | tf_op jit(solution)/shard_map/ppermute | solution.py:435
  25.5 30.2 %collective-permute-start.1 = (bf16[64,4096]{1,0:T(8,128)(2,1)}, bf16[64,4096]{1,0:T(8,128)(2,1)S(1)}, u32[]{:S(2)}, u32[]{:S(2)}) collective-permute-start(bf16[64,4096]{1,0:T(8,128)(2,1)} %get-tuple-element.63), channel_id=1, source_target_pairs={{0,1},{1,2},{2,3},{3,0},{4,5},{5,6},{6,7},{7,4},{8,9},{9,10},{10,1... | collective-permute-start | bytes 1572872 | tf_op jit(solution)/shard_map/ppermute | solution.py:425
  26.8 28.9 %collective-permute-start.2 = (bf16[64,4096]{1,0:T(8,128)(2,1)}, bf16[64,4096]{1,0:T(8,128)(2,1)S(1)}, u32[]{:S(2)}, u32[]{:S(2)}) collective-permute-start(bf16[64,4096]{1,0:T(8,128)(2,1)} %get-tuple-element.64), channel_id=1, source_target_pairs={{0,3},{1,0},{2,1},{3,2},{4,7},{5,4},{6,5},{7,6},{8,11},{9,8},{10,9... | collective-permute-start | bytes 1572872 | tf_op jit(solution)/shard_map/ppermute | solution.py:426
  28.2 6.9 %collective-permute-start.12 = (bf16[512,256]{1,0:T(8,128)(2,1)}, bf16[512,256]{1,0:T(8,128)(2,1)}, u32[]{:S(2)}, u32[]{:S(2)}) collective-permute-start(bf16[512,256]{1,0:T(8,128)(2,1)} %collective-permute-done.6.refs_1_), channel_id=1, source_target_pairs={{0,4},{4,8},{8,12},{12,0},{16,20},{20,24},{24,28},{28,16},{1,5},{5... | collective-permute-start | bytes 786440 | tf_op jit(solution)/shard_map/ppermute | solution.py:434
  29.0 26.8 %collective-permute-start.4 = (bf16[64,4096]{1,0:T(8,128)(2,1)S(1)}, bf16[64,4096]{1,0:T(8,128)(2,1)S(1)}, u32[]{:S(2)}, u32[]{:S(2)}) collective-permute-start(bf16[64,4096]{1,0:T(8,128)(2,1)S(1)} %collective-permute-done.refs_1_), channel_id=1, source_target_pairs={{0,1},{1,2},{2,3},{3,0},{4,5},{5,6},{6,7},{7,4},{8,9},{9,10},{10,1... | collective-permute-start | bytes 1572872 | tf_op jit(solution)/shard_map/ppermute | solution.py:423
  31.6 24.1 %collective-permute-start.5 = (bf16[64,4096]{1,0:T(8,128)(2,1)S(1)}, bf16[64,4096]{1,0:T(8,128)(2,1)S(1)}, u32[]{:S(2)}, u32[]{:S(2)}) collective-permute-start(bf16[64,4096]{1,0:T(8,128)(2,1)S(1)} %collective-permute-done.3.refs_4_), channel_id=1, source_target_pairs={{0,3},{1,0},{2,1},{3,2},{4,7},{5,4},{6,5},{7,6},{8,11},{9,8},{10,9... | collective-permute-start | bytes 1572872 | tf_op jit(solution)/shard_map/ppermute | solution.py:424
  35.2 126.1 %collective-permute-start.23 = (bf16[4096,256]{1,0:T(8,128)(2,1)}, bf16[4096,256]{1,0:T(8,128)(2,1)}, u32[]{:S(2)}, u32[]{:S(2)}) collective-permute-start(bf16[4096,256]{1,0:T(8,128)(2,1)} %pad_maximum_fusion), channel_id=1, source_target_pairs={{0,96},{32,0},{64,32},{96,64},{1,97},{33,1},{65,33},{97,65},{2,98}... | collective-permute-start | bytes 6291464 | tf_op jit(solution)/shard_map/ppermute | solution.py:442
  81.5 6.1 %collective-permute-start.26 = (bf16[2,128,128]{2,1,0:T(8,128)(2,1)S(1)}, bf16[2,128,128]{2,1,0:T(8,128)(2,1)S(1)}, u32[]{:S(2)}, u32[]{:S(2)}) collective-permute-start(bf16[2,128,128]{2,1,0:T(8,128)(2,1)S(1)} %get-tuple-element.57), channel_id=1, source_target_pairs={{0,12},{4,0},{8,4},{12,8},{16,28},{20,16},{24,20},{28,24},{1,13},{... | collective-permute-start | bytes 196616 | tf_op jit(solution)/shard_map/ppermute | solution.py:465
  81.8 6.8 %collective-permute-start.25 = (bf16[2,128,128]{2,1,0:T(8,128)(2,1)S(1)}, bf16[2,128,128]{2,1,0:T(8,128)(2,1)S(1)}, u32[]{:S(2)}, u32[]{:S(2)}) collective-permute-start(bf16[2,128,128]{2,1,0:T(8,128)(2,1)S(1)} %get-tuple-element.56), channel_id=1, source_target_pairs={{0,8},{4,12},{8,0},{12,4},{16,24},{20,28},{24,16},{28,20},{1,9},{5... | collective-permute-start | bytes 196616 | tf_op jit(solution)/shard_map/ppermute | solution.py:465
  85.4 24.6 %collective-permute-start.20 = (bf16[2,512,128]{2,1,0:T(8,128)(2,1)S(1)}, bf16[2,512,128]{2,1,0:T(8,128)(2,1)S(1)}, u32[]{:S(2)}, u32[]{:S(2)}) collective-permute-start(bf16[2,512,128]{2,1,0:T(8,128)(2,1)S(1)} %get-tuple-element.50), channel_id=1, source_target_pairs={{0,12},{4,0},{8,4},{12,8},{16,28},{20,16},{24,20},{28,24},{1,13},{... | collective-permute-start | bytes 786440 | tf_op jit(solution)/shard_map/ppermute | solution.py:465
  87.6 9.4 %collective-permute-start.16 = (bf16[2,384,128]{2,1,0:T(8,128)(2,1)S(1)}, bf16[2,384,128]{2,1,0:T(8,128)(2,1)S(1)}, u32[]{:S(2)}, u32[]{:S(2)}) collective-permute-start(bf16[2,384,128]{2,1,0:T(8,128)(2,1)S(1)} %get-tuple-element.46), channel_id=1, source_target_pairs={{0,12},{4,0},{8,4},{12,8},{16,28},{20,16},{24,20},{28,24},{1,13},{... | collective-permute-start | bytes 589832 | tf_op jit(solution)/shard_map/ppermute | solution.py:465
  88.7 11.0 %collective-permute-start.15 = (bf16[2,384,128]{2,1,0:T(8,128)(2,1)S(1)}, bf16[2,384,128]{2,1,0:T(8,128)(2,1)S(1)}, u32[]{:S(2)}, u32[]{:S(2)}) collective-permute-start(bf16[2,384,128]{2,1,0:T(8,128)(2,1)S(1)} %get-tuple-element.45), channel_id=1, source_target_pairs={{0,8},{4,12},{8,0},{12,4},{16,24},{20,28},{24,16},{28,20},{1,9},{5... | collective-permute-start | bytes 589832 | tf_op jit(solution)/shard_map/ppermute | solution.py:465
  93.1 10.1 %collective-permute-start.14 = (bf16[2,384,128]{2,1,0:T(8,128)(2,1)S(1)}, bf16[2,384,128]{2,1,0:T(8,128)(2,1)S(1)}, u32[]{:S(2)}, u32[]{:S(2)}) collective-permute-start(bf16[2,384,128]{2,1,0:T(8,128)(2,1)S(1)} %get-tuple-element.44), channel_id=1, source_target_pairs={{0,4},{4,8},{8,12},{12,0},{16,20},{20,24},{24,28},{28,16},{1,5},{5... | collective-permute-start | bytes 589832 | tf_op jit(solution)/shard_map/ppermute | solution.py:465
  97.0 13.1 %collective-permute-start.19 = (bf16[2,512,128]{2,1,0:T(8,128)(2,1)S(1)}, bf16[2,512,128]{2,1,0:T(8,128)(2,1)S(1)}, u32[]{:S(2)}, u32[]{:S(2)}) collective-permute-start(bf16[2,512,128]{2,1,0:T(8,128)(2,1)S(1)} %get-tuple-element.49), channel_id=1, source_target_pairs={{0,8},{4,12},{8,0},{12,4},{16,24},{20,28},{24,16},{28,20},{1,9},{5... | collective-permute-start | bytes 786440 | tf_op jit(solution)/shard_map/ppermute | solution.py:465
  99.6 10.5 %collective-permute-start.18 = (bf16[2,512,128]{2,1,0:T(8,128)(2,1)S(1)}, bf16[2,512,128]{2,1,0:T(8,128)(2,1)S(1)}, u32[]{:S(2)}, u32[]{:S(2)}) collective-permute-start(bf16[2,512,128]{2,1,0:T(8,128)(2,1)S(1)} %get-tuple-element.48), channel_id=1, source_target_pairs={{0,4},{4,8},{8,12},{12,0},{16,20},{20,24},{24,28},{28,16},{1,5},{5... | collective-permute-start | bytes 786440 | tf_op jit(solution)/shard_map/ppermute | solution.py:465
  103.2 55.0 %collective-permute-start.13 = (bf16[128,4096]{1,0:T(8,128)(2,1)S(1)}, bf16[128,4096]{1,0:T(8,128)(2,1)S(1)}, u32[]{:S(2)}, u32[]{:S(2)}) collective-permute-start(bf16[128,4096]{1,0:T(8,128)(2,1)S(1)} %convolution_convert_fusion), channel_id=1, source_target_pairs={{0,96},{32,0},{64,32},{96,64},{1,97},{33,1},{65,33},{97,65},{2,98}... | collective-permute-start | bytes 3145736 | tf_op jit(solution)/shard_map/ppermute | solution.py:492
  110.0 6.1 %collective-permute-start.17 = (bf16[384,128]{1,0:T(8,128)(2,1)S(1)}, bf16[384,128]{1,0:T(8,128)(2,1)S(1)}, u32[]{:S(2)}, u32[]{:S(2)}) collective-permute-start(bf16[384,128]{1,0:T(8,128)(2,1)S(1)} %fusion.31), channel_id=1, source_target_pairs={{0,16},{4,20},{8,24},{12,28},{16,0},{20,4},{24,8},{28,12},{1,17},{... | collective-permute-start | bytes 294920 | tf_op jit(solution)/shard_map/ppermute | solution.py:481
  110.3 9.4 %collective-permute-start.21 = (bf16[512,128]{1,0:T(8,128)(2,1)S(1)}, bf16[512,128]{1,0:T(8,128)(2,1)S(1)}, u32[]{:S(2)}, u32[]{:S(2)}) collective-permute-start(bf16[512,128]{1,0:T(8,128)(2,1)S(1)} %fusion.26), channel_id=1, source_target_pairs={{0,16},{4,20},{8,24},{12,28},{16,0},{20,4},{24,8},{28,12},{1,17},{... | collective-permute-start | bytes 393224 | tf_op jit(solution)/shard_map/ppermute | solution.py:481
  120.7 12.5 %collective-permute-start.28 = (bf16[64,4096]{1,0:T(8,128)(2,1)S(1)}, bf16[64,4096]{1,0:T(8,128)(2,1)S(1)}, u32[]{:S(2)}, u32[]{:S(2)}) collective-permute-start(bf16[64,4096]{1,0:T(8,128)(2,1)S(1)} %get-tuple-element.61), channel_id=1, source_target_pairs={{0,1},{1,2},{2,3},{3,0},{4,5},{5,6},{6,7},{7,4},{8,9},{9,10},{10,1... | collective-permute-start | bytes 1572872 | tf_op jit(solution)/shard_map/ppermute | solution.py:512
  122.9 40.8 %collective-permute-start.30 = (bf16[64,4096]{1,0:T(8,128)(2,1)S(1)}, bf16[64,4096]{1,0:T(8,128)(2,1)S(1)}, u32[]{:S(2)}, u32[]{:S(2)}) collective-permute-start(bf16[64,4096]{1,0:T(8,128)(2,1)S(1)} %slice.102), channel_id=1, source_target_pairs={{0,99},{1,96},{2,97},{3,98},{32,3},{33,0},{34,1},{35,2},{64,35},{6... | collective-permute-start | bytes 1572872 | tf_op jit(solution)/shard_map/ppermute | solution.py:517
  133.1 22.4 %collective-permute-start.22 = (bf16[128,256]{1,0:T(8,128)(2,1)S(1)}, bf16[128,256]{1,0:T(8,128)(2,1)S(1)}, u32[]{:S(2)}, u32[]{:S(2)}) collective-permute-start(bf16[128,256]{1,0:T(8,128)(2,1)S(1)} %pad_maximum_fusion.3), channel_id=1, source_target_pairs={{0,96},{32,0},{64,32},{96,64},{1,97},{33,1},{65,33},{97,65},{2,98}... | collective-permute-start | bytes 196616 | tf_op jit(solution)/shard_map/ppermute | solution.py:518
  133.3 22.2 %collective-permute-start.32 = (bf16[64,4096]{1,0:T(8,128)(2,1)S(1)}, bf16[64,4096]{1,0:T(8,128)(2,1)S(1)}, u32[]{:S(2)}, u32[]{:S(2)}) collective-permute-start(bf16[64,4096]{1,0:T(8,128)(2,1)S(1)} %get-tuple-element.62), channel_id=1, source_target_pairs={{0,3},{1,0},{2,1},{3,2},{4,7},{5,4},{6,5},{7,6},{8,11},{9,8},{10,9... | collective-permute-start | bytes 1572872 | tf_op jit(solution)/shard_map/ppermute | solution.py:513
  155.4 17.4 %collective-permute-start.31 = (bf16[64,4096]{1,0:T(8,128)(2,1)S(1)}, bf16[64,4096]{1,0:T(8,128)(2,1)S(1)}, u32[]{:S(2)}, u32[]{:S(2)}) collective-permute-start(bf16[64,4096]{1,0:T(8,128)(2,1)S(1)} %slice.104), channel_id=1, source_target_pairs={{0,97},{1,98},{2,99},{3,96},{32,1},{33,2},{34,3},{35,0},{64,33},{6... | collective-permute-start | bytes 1572872 | tf_op jit(solution)/shard_map/ppermute | solution.py:516
  155.6 22.8 %collective-permute-start.29 = (bf16[64,4096]{1,0:T(8,128)(2,1)S(1)}, bf16[64,4096]{1,0:T(8,128)(2,1)S(1)}, u32[]{:S(2)}, u32[]{:S(2)}) collective-permute-start(bf16[64,4096]{1,0:T(8,128)(2,1)S(1)} %add_convert_fusion.1), channel_id=1, source_target_pairs={{0,97},{1,98},{2,99},{3,96},{32,1},{33,2},{34,3},{35,0},{64,33},{6... | collective-permute-start | bytes 1572872 | tf_op jit(solution)/shard_map/ppermute | solution.py:521
  158.3 20.2 %collective-permute-start.33 = (bf16[64,4096]{1,0:T(8,128)(2,1)S(1)}, bf16[64,4096]{1,0:T(8,128)(2,1)S(1)}, u32[]{:S(2)}, u32[]{:S(2)}) collective-permute-start(bf16[64,4096]{1,0:T(8,128)(2,1)S(1)} %add_convert_fusion), channel_id=1, source_target_pairs={{0,99},{1,96},{2,97},{3,98},{32,3},{33,0},{34,1},{35,2},{64,35},{6... | collective-permute-start | bytes 1572872 | tf_op jit(solution)/shard_map/ppermute | solution.py:523
  (22 other events, 113.1 us)
where the time goes:
time: 182 us; the launch traced here: 180 us
  starting transfers between devices  67 us (37%)
  waiting for transfers between devices  47.5 us (26%)
  Pallas kernels  33.3 us (18%)
  local copies, waits for them, and re-layouts  12.5 us (7%)
  matrix products  10.8 us (6%)
  other arithmetic  7.6 us (4%)
    ppermute x1, waiting for transfers between devices, per_device(): from_right = send(far[half_rows:], TP, ring(4, -1))  21.6 us
    ppermute x9, starting transfers between devices, along_z(): received = send(groups[distance], CTX, z_ring(shift))  12.6 us
    pallas_call x1, Pallas kernels, key_call(): pl.pallas_call(key_kernel, grid_spec=pltpu.PrefetchScalarGridSpec(num_sca...  12.1 us
    pallas_call x1, Pallas kernels, forward_call(): pl.pallas_call(forward_kernel, grid_spec=pltpu.PrefetchScalarGridSpec(num...  10.9 us
    dot_general x8, matrix products, dot_nt(): lax.dot_general(lhs, rhs, (((1,), (1,)), ((), ())), preferred_element_typ...  10.8 us
    ppermute x1, starting transfers between devices, per_device(): top_b = send(left[:half_rows], joint, joint_ring(-1))  10.3 us
    unnamed x41, local copies, waits for them, and re-layouts  9.51 us
    ppermute x1, waiting for transfers between devices, per_device(): low_a = send(right[half_rows:], joint, joint_ring(1))  9.08 us
  transfers between devices with their start and end apart: 34, of which 9 were waited for; matrix products, arithmetic and copies ran while one was open for 11% of the time, Pallas kernels for 19%

commit v1 on v0

--- a/solution.py
+++ b/solution.py
@@ -189,7 +189,7 @@
 
 
 def grad_call(rows, pieces, out_weight):
-    depth = 1024
+    depth = 2048
     total = out_weight.shape[0]
     return pl.pallas_call(
         grad_kernel,
@@ -487,7 +487,8 @@
     query_terms = []
     for distance in range(4):
         query_terms.append(dot_nt(chunk_of(query_grad, distance), query_weight[0]))
-    query_terms[0] = query_terms[0].astype(bf16)
+    for distance in (0, 1, 3):
+        query_terms[distance] = query_terms[distance].astype(bf16)
     query_terms = [lax.optimization_barrier(term) for term in query_terms]
     own = send(query_terms[0], SECTION, ring(4, -1))
 

time: 182 us -> 182 us (level)
  transfers between devices with their start and end apart: 34 -> 34, of which waited for: 9 -> 9; matrix products, arithmetic and copies ran while one was open for 11% -> 11% of each run, Pallas kernels for 19% -> 18%
where the time goes in v1:
time: 182 us; the launch traced here: 179 us
  starting transfers between devices  66.9 us (37%)
  waiting for transfers between devices  47.6 us (26%)
  Pallas kernels  32.9 us (18%)
  local copies, waits for them, and re-layouts  12.5 us (7%)
  matrix products  10.8 us (6%)
  other arithmetic  7.61 us (4%)
    ppermute x1, waiting for transfers between devices, per_device(): from_right = send(far[half_rows:], TP, ring(4, -1))  21.7 us
    ppermute x9, starting transfers between devices, along_z(): received = send(groups[distance], CTX, z_ring(shift))  12.5 us
    pallas_call x1, Pallas kernels, key_call(): pl.pallas_call(key_kernel, grid_spec=pltpu.PrefetchScalarGridSpec(num_sca...  12.1 us
    pallas_call x1, Pallas kernels, forward_call(): pl.pallas_call(forward_kernel, grid_spec=pltpu.PrefetchScalarGridSpec(num...  10.9 us
    dot_general x8, matrix products, dot_nt(): lax.dot_general(lhs, rhs, (((1,), (1,)), ((), ())), preferred_element_typ...  10.8 us
    ppermute x1, starting transfers between devices, per_device(): top_b = send(left[:half_rows], joint, joint_ring(-1))  10.3 us
    unnamed x41, local copies, waits for them, and re-layouts  9.51 us
    ppermute x1, waiting for transfers between devices, per_device(): low_a = send(right[half_rows:], joint, joint_ring(1))  9.09 us
  transfers between devices with their start and end apart: 34, of which 9 were waited for; matrix products, arithmetic and copies ran while one was open for 11% of the time, Pallas kernels for 18%

profile of v1, /device:TPU:1, one launch (start us, length us, event | category | flops | bytes accessed | tf_op | source)
XLA Modules:
  0.0 179.4 jit_solution(2782909662054154387)
XLA Ops:
  1.8 3.6 %collective-permute-start.6 = (bf16[512,256]{1,0:T(8,128)(2,1)S(1)}, bf16[512,256]{1,0:T(8,128)(2,1)}, u32[]{:S(2)}, u32[]{:S(2)}) collective-permute-start(bf16[512,256]{1,0:T(8,128)(2,1)S(1)} %pad_maximum_fusion.2.refs_0_), channel_id=1, source_target_pairs={{0,16},{4,20},{8,24},{12,28},{16,0},{20,4},{24,8},{28,12},{1,17},{... | collective-permute-start | bytes 786440 | tf_op jit(solution)/shard_map/ppermute | solution.py:429
  5.4 3.8 %collective-permute-start.7 = (bf16[512,256]{1,0:T(8,128)(2,1)S(1)}, bf16[512,256]{1,0:T(8,128)(2,1)S(1)}, u32[]{:S(2)}, u32[]{:S(2)}) collective-permute-start(bf16[512,256]{1,0:T(8,128)(2,1)S(1)} %pad_maximum_fusion.2.refs_0_), channel_id=1, source_target_pairs={{0,12},{4,0},{8,4},{12,8},{16,28},{20,16},{24,20},{28,24},{1,13},{... | collective-permute-start | bytes 786440 | tf_op jit(solution)/shard_map/ppermute | solution.py:432
  9.2 2.3 %slice_bitcast_fusion = (bf16[64,4096]{1,0:T(8,128)(2,1)}, bf16[64,4096]{1,0:T(8,128)(2,1)}) fusion(bf16[1,128,4096]{2,1,0:T(8,128)(2,1)} %param.13), kind=kLoop, calls=%fused_computation.28 | loop fusion | bytes 2097152 | tf_op jit(solution)/shard_map/slice | solution.py:420
  14.2 1.6 pad_maximum_fusion
  16.6 2.8 %collective-permute-done.7.refs_2_ = bf16[512,256]{1,0:T(8,128)(2,1)S(1)} collective-permute-done((bf16[512,256]{1,0:T(8,128)(2,1)S(1)}, bf16[512,256]{1,0:T(8,128)(2,1)S(1)}, u32[]{:S(2)}, u32[]{:S(2)}) %collective-permute-start.7) | collective-permute-done | bytes 262176 | tf_op jit(solution)/shard_map/ppermute | solution.py:432
  20.1 3.6 %collective-permute-start.8 = (bf16[512,256]{1,0:T(8,128)(2,1)}, bf16[512,256]{1,0:T(8,128)(2,1)S(1)}, u32[]{:S(2)}, u32[]{:S(2)}) collective-permute-start(bf16[512,256]{1,0:T(8,128)(2,1)} %collective-permute-done.6.refs_1_), channel_id=1, source_target_pairs={{0,12},{4,0},{8,4},{12,8},{16,28},{20,16},{24,20},{28,24},{1,13},{... | collective-permute-start | bytes 786440 | tf_op jit(solution)/shard_map/ppermute | solution.py:434
  26.8 1.4 collective-permute-start.2
  31.6 2.7 %collective-permute-start.5 = (bf16[64,4096]{1,0:T(8,128)(2,1)S(1)}, bf16[64,4096]{1,0:T(8,128)(2,1)S(1)}, u32[]{:S(2)}, u32[]{:S(2)}) collective-permute-start(bf16[64,4096]{1,0:T(8,128)(2,1)S(1)} %collective-permute-done.3.refs_4_), channel_id=1, source_target_pairs={{0,3},{1,0},{2,1},{3,2},{4,7},{5,4},{6,5},{7,6},{8,11},{9,8},{10,9... | collective-permute-start | bytes 1572872 | tf_op jit(solution)/shard_map/ppermute | solution.py:424
  35.2 3.8 %collective-permute-start.23 = (bf16[4096,256]{1,0:T(8,128)(2,1)}, bf16[4096,256]{1,0:T(8,128)(2,1)}, u32[]{:S(2)}, u32[]{:S(2)}) collective-permute-start(bf16[4096,256]{1,0:T(8,128)(2,1)} %pad_maximum_fusion), channel_id=1, source_target_pairs={{0,96},{32,0},{64,32},{96,64},{1,97},{33,1},{65,33},{97,65},{2,98}... | collective-permute-start | bytes 6291464 | tf_op jit(solution)/shard_map/ppermute | solution.py:442
  44.8 10.9 %shard_map.113 = (bf16[17,4,256,256]{3,2,1,0:T(8,128)(2,1)S(1)}, f32[2,128,1024]{2,1,0:T(8,128)S(1)}, f32[2,8,1024]{2,1,0:T(8,128)S(1)}, f32[17,1,1024]{2,1,0:T(1,128)S(1)}, bf16[16,256,256]{2,1,0:T(8,128)(2,1)S(1)}) custom-call(s32[1]{0:T(128)S(1)} %bitcast.73, s32[16]{0:T(128)S(1)} %reshape.116.ids_ref, bf16[512,256]{1,0:T(8,128)(2,1)S(1)} %pad_maximum_fusion.2.refs_0_, ...), custom_call_target="tpu_custom_call" | custom-call | flops 2281701376 | bytes 13631488 | tf_op jit(solution)/shard_map/pallas_call | solution.py:131
  55.8 3.8 %shard_map.112.grad_ref = bf16[512,512]{1,0:T(8,128)(2,1)S(1)} custom-call(s32[7]{0:T(128)S(1)} %broadcast_multiply_fusion.rows_ref, bf16[128,4096]{1,0:T(8,128)(2,1)S(1)} %bitcast.69, bf16[64,4096]{1,0:T(8,128)(2,1)S(1)} %collective-permute-done.refs_1_, bf16[64,4096]{1,0:T(8,128)(2,1)S(1)} %collective-permute-done.1.refs_2_, ...), custom_call_target="tpu_custom_call" | custom-call | flops 2147483648 | bytes 9437184 | tf_op jit(solution)/shard_map/pallas_call | solution.py:194
  59.5 6.2 %attn_value_grad.1 = (bf16[2,512,128]{2,1,0:T(8,128)(2,1)S(1)}, bf16[2,512,128]{2,1,0:T(8,128)(2,1)S(1)}, bf16[2,512,128]{2,1,0:T(8,128)(2,1)S(1)}, bf16[2,512,128]{2,1,0:T(8,128)(2,1)S(1)}) custom-call(s32[1]{0:T(128)S(1)} %bitcast.74, s32[16]{0:T(128)S(1)} %reshape.116.ids_ref, s32[4]{0:T(128)S(1)} %pad_add_fusion.chunk_ref, ...), custom_call_target="tpu_custom_call" | custom-call | flops 1140850688 | bytes 11534336 | tf_op jit(solution)/shard_map/attn_value_grad/pallas_call | solution.py:260
  65.7 12.1 %shard_map.114 = (bf16[512,512]{1,0:T(8,128)(2,1)S(1)}, bf16[2,128,128]{2,1,0:T(8,128)(2,1)S(1)}, bf16[2,128,128]{2,1,0:T(8,128)(2,1)S(1)}, bf16[2,128,128]{2,1,...) custom-call(s32[1]{0:T(128)S(1)} %bitcast.75, ...), custom_call_target="tpu_custom_call" | custom-call | flops 3422552064 | bytes 14680064 | tf_op jit(solution)/shard_map/pallas_call | solution.py:367
  78.1 1.5 convolution_convert_fusion.1
  79.6 1.5 fusion.3
  83.5 1.5 convolution_convert_fusion.2
  85.0 2.2 %collective-permute-start.20 = (bf16[2,512,128]{2,1,0:T(8,128)(2,1)S(1)}, bf16[2,512,128]{2,1,0:T(8,128)(2,1)S(1)}, u32[]{:S(2)}, u32[]{:S(2)}) collective-permute-start(bf16[2,512,128]{2,1,0:T(8,128)(2,1)S(1)} %get-tuple-element.50), channel_id=1, source_target_pairs={{0,12},{4,0},{8,4},{12,8},{16,28},{20,16},{24,20},{28,24},{1,13},{... | collective-permute-start | bytes 786440 | tf_op jit(solution)/shard_map/ppermute | solution.py:465
  88.4 2.8 %collective-permute-start.27 = (bf16[128,128]{1,0:T(8,128)(2,1)S(1)}, bf16[128,128]{1,0:T(8,128)(2,1)S(1)}, u32[]{:S(2)}, u32[]{:S(2)}) collective-permute-start(bf16[128,128]{1,0:T(8,128)(2,1)S(1)} %fusion.41), channel_id=1, source_target_pairs={{0,16},{4,20},{8,24},{12,28},{16,0},{20,4},{24,8},{28,12},{1,17},{... | collective-permute-start | bytes 98312 | tf_op jit(solution)/shard_map/ppermute | solution.py:481
  91.2 1.5 convolution_convert_fusion
  93.6 3.0 %collective-permute-done.16 = bf16[2,384,128]{2,1,0:T(8,128)(2,1)S(1)} collective-permute-done((bf16[2,384,128]{2,1,0:T(8,128)(2,1)S(1)}, bf16[2,384,128]{2,1,0:T(8,128)(2,1)S(1)}, u32[]{:S(2)}, u32[]{:S(2)}) %collective-permute-start.16) | collective-permute-done | bytes 196640 | tf_op jit(solution)/shard_map/ppermute | solution.py:465
  96.6 2.5 %collective-permute-start.19 = (bf16[2,512,128]{2,1,0:T(8,128)(2,1)S(1)}, bf16[2,512,128]{2,1,0:T(8,128)(2,1)S(1)}, u32[]{:S(2)}, u32[]{:S(2)}) collective-permute-start(bf16[2,512,128]{2,1,0:T(8,128)(2,1)S(1)} %get-tuple-element.49), channel_id=1, source_target_pairs={{0,8},{4,12},{8,0},{12,4},{16,24},{20,28},{24,16},{28,20},{1,9},{5... | collective-permute-start | bytes 786440 | tf_op jit(solution)/shard_map/ppermute | solution.py:465
  99.2 3.6 %collective-permute-start.18 = (bf16[2,512,128]{2,1,0:T(8,128)(2,1)S(1)}, bf16[2,512,128]{2,1,0:T(8,128)(2,1)S(1)}, u32[]{:S(2)}, u32[]{:S(2)}) collective-permute-start(bf16[2,512,128]{2,1,0:T(8,128)(2,1)S(1)} %get-tuple-element.48), channel_id=1, source_target_pairs={{0,4},{4,8},{8,12},{12,0},{16,20},{20,24},{24,28},{28,16},{1,5},{5... | collective-permute-start | bytes 786440 | tf_op jit(solution)/shard_map/ppermute | solution.py:465
  102.8 6.7 %collective-permute-start.13 = (bf16[128,4096]{1,0:T(8,128)(2,1)S(1)}, bf16[128,4096]{1,0:T(8,128)(2,1)S(1)}, u32[]{:S(2)}, u32[]{:S(2)}) collective-permute-start(bf16[128,4096]{1,0:T(8,128)(2,1)S(1)} %convolution_convert_fusion.2), channel_id=1, source_target_pairs={{0,96},{32,0},{64,32},{96,64},{1,97},{33,1},{65,33},{97,65},{2,98}... | collective-permute-start | bytes 3145736 | tf_op jit(solution)/shard_map/ppermute | solution.py:493
  109.9 5.7 %collective-permute-start.21 = (bf16[512,128]{1,0:T(8,128)(2,1)S(1)}, bf16[512,128]{1,0:T(8,128)(2,1)S(1)}, u32[]{:S(2)}, u32[]{:S(2)}) collective-permute-start(bf16[512,128]{1,0:T(8,128)(2,1)S(1)} %fusion.24), channel_id=1, source_target_pairs={{0,16},{4,20},{8,24},{12,28},{16,0},{20,4},{24,8},{28,12},{1,17},{... | collective-permute-start | bytes 393224 | tf_op jit(solution)/shard_map/ppermute | solution.py:481
  115.8 3.6 %collective-permute-done.21 = bf16[512,128]{1,0:T(8,128)(2,1)S(1)} collective-permute-done((bf16[512,128]{1,0:T(8,128)(2,1)S(1)}, bf16[512,128]{1,0:T(8,128)(2,1)S(1)}, u32[]{:S(2)}, u32[]{:S(2)}) %collective-permute-start.21) | collective-permute-done | bytes 131104 | tf_op jit(solution)/shard_map/ppermute | solution.py:481
  122.4 10.3 %collective-permute-start.30 = (bf16[64,4096]{1,0:T(8,128)(2,1)S(1)}, bf16[64,4096]{1,0:T(8,128)(2,1)S(1)}, u32[]{:S(2)}, u32[]{:S(2)}) collective-permute-start(bf16[64,4096]{1,0:T(8,128)(2,1)S(1)} %slice.102), channel_id=1, source_target_pairs={{0,99},{1,96},{2,97},{3,98},{32,3},{33,0},{34,1},{35,2},{64,35},{6... | collective-permute-start | bytes 1572872 | tf_op jit(solution)/shard_map/ppermute | solution.py:518
  133.3 21.7 %collective-permute-done.32 = bf16[64,4096]{1,0:T(8,128)(2,1)S(1)} collective-permute-done((bf16[64,4096]{1,0:T(8,128)(2,1)S(1)}, bf16[64,4096]{1,0:T(8,128)(2,1)S(1)}, u32[]{:S(2)}, u32[]{:S(2)}) %collective-permute-start.32) | collective-permute-done | bytes 524320 | tf_op jit(solution)/shard_map/ppermute | solution.py:514
  155.1 2.7 %collective-permute-start.29 = (bf16[64,4096]{1,0:T(8,128)(2,1)S(1)}, bf16[64,4096]{1,0:T(8,128)(2,1)S(1)}, u32[]{:S(2)}, u32[]{:S(2)}) collective-permute-start(bf16[64,4096]{1,0:T(8,128)(2,1)S(1)} %add_convert_fusion.1), channel_id=1, source_target_pairs={{0,97},{1,98},{2,99},{3,96},{32,1},{33,2},{34,3},{35,0},{64,33},{6... | collective-permute-start | bytes 1572872 | tf_op jit(solution)/shard_map/ppermute | solution.py:522
  158.3 1.4 fusion.23
  160.8 2.4 %convert_add_fusion = f32[128,4096]{1,0:T(8,128)S(1)} fusion(bf16[128,4096]{1,0:T(8,128)(2,1)S(1)} %collective-permute-done.13, bf16[128,256]{1,0:T(8,128)(2,1)S(1)} %collective-permute-done.22, bf16[4096,256]{1,0:T(8,128)(2,1)} %collective-permute-done.23), kind=kOutput, calls=%fused_computation.15 | convolution fusion | flops 269484032 | bytes 5308416 | tf_op jit(solution)/shard_map/dot_general | solution.py:22
  163.3 9.1 %collective-permute-done.31 = bf16[64,4096]{1,0:T(8,128)(2,1)S(1)} collective-permute-done((bf16[64,4096]{1,0:T(8,128)(2,1)S(1)}, bf16[64,4096]{1,0:T(8,128)(2,1)S(1)}, u32[]{:S(2)}, u32[]{:S(2)}) %collective-permute-start.31) | collective-permute-done | bytes 524320 | tf_op jit(solution)/shard_map/ppermute | solution.py:517
  172.4 5.6 %collective-permute-done.29 = bf16[64,4096]{1,0:T(8,128)(2,1)S(1)} collective-permute-done((bf16[64,4096]{1,0:T(8,128)(2,1)S(1)}, bf16[64,4096]{1,0:T(8,128)(2,1)S(1)}, u32[]{:S(2)}, u32[]{:S(2)}) %collective-permute-start.29) | collective-permute-done | bytes 524320 | tf_op jit(solution)/shard_map/ppermute | solution.py:522
  (122 shorter events, 30.6 us)
Async XLA Ops:
  1.8 14.0 %collective-permute-start.6 = (bf16[512,256]{1,0:T(8,128)(2,1)S(1)}, bf16[512,256]{1,0:T(8,128)(2,1)}, u32[]{:S(2)}, u32[]{:S(2)}) collective-permute-start(bf16[512,256]{1,0:T(8,128)(2,1)S(1)} %pad_maximum_fusion.2.refs_0_), channel_id=1, source_target_pairs={{0,16},{4,20},{8,24},{12,28},{16,0},{20,4},{24,8},{28,12},{1,17},{... | collective-permute-start | bytes 786440 | tf_op jit(solution)/shard_map/ppermute | solution.py:429
  5.4 13.9 %collective-permute-start.7 = (bf16[512,256]{1,0:T(8,128)(2,1)S(1)}, bf16[512,256]{1,0:T(8,128)(2,1)S(1)}, u32[]{:S(2)}, u32[]{:S(2)}) collective-permute-start(bf16[512,256]{1,0:T(8,128)(2,1)S(1)} %pad_maximum_fusion.2.refs_0_), channel_id=1, source_target_pairs={{0,12},{4,0},{8,4},{12,8},{16,28},{20,16},{24,20},{28,24},{1,13},{... | collective-permute-start | bytes 786440 | tf_op jit(solution)/shard_map/ppermute | solution.py:432
  9.2 14.4 %collective-permute-start.9 = (bf16[512,256]{1,0:T(8,128)(2,1)S(1)}, bf16[512,256]{1,0:T(8,128)(2,1)S(1)}, u32[]{:S(2)}, u32[]{:S(2)}) collective-permute-start(bf16[512,256]{1,0:T(8,128)(2,1)S(1)} %pad_maximum_fusion.2.refs_0_), channel_id=1, source_target_pairs={{0,8},{4,12},{8,0},{12,4},{16,24},{20,28},{24,16},{28,20},{1,9},{5... | collective-permute-start | bytes 786440 | tf_op jit(solution)/shard_map/ppermute | solution.py:432
  11.5 15.3 %collective-permute-start = (bf16[64,4096]{1,0:T(8,128)(2,1)}, bf16[64,4096]{1,0:T(8,128)(2,1)S(1)}, u32[]{:S(2)}, u32[]{:S(2)}) collective-permute-start(bf16[64,4096]{1,0:T(8,128)(2,1)} %get-tuple-element.64), channel_id=1, source_target_pairs={{0,1},{1,2},{2,3},{3,0},{4,5},{5,6},{6,7},{7,4},{8,9},{9,10},{10,1... | collective-permute-start | bytes 1572872 | tf_op jit(solution)/shard_map/ppermute | solution.py:421
  12.8 15.5 %collective-permute-start.3 = (bf16[64,4096]{1,0:T(8,128)(2,1)}, bf16[64,4096]{1,0:T(8,128)(2,1)S(1)}, u32[]{:S(2)}, u32[]{:S(2)}) collective-permute-start(bf16[64,4096]{1,0:T(8,128)(2,1)} %get-tuple-element.63), channel_id=1, source_target_pairs={{0,3},{1,0},{2,1},{3,2},{4,7},{5,4},{6,5},{7,6},{8,11},{9,8},{10,9... | collective-permute-start | bytes 1572872 | tf_op jit(solution)/shard_map/ppermute | solution.py:422
  15.8 9.0 %collective-permute-start.11 = (bf16[512,256]{1,0:T(8,128)(2,1)S(1)}, bf16[512,256]{1,0:T(8,128)(2,1)S(1)}, u32[]{:S(2)}, u32[]{:S(2)}) collective-permute-start(bf16[512,256]{1,0:T(8,128)(2,1)S(1)} %pad_maximum_fusion.2.refs_0_), channel_id=1, source_target_pairs={{0,4},{4,8},{8,12},{12,0},{16,20},{20,24},{24,28},{28,16},{1,5},{5... | collective-permute-start | bytes 786440 | tf_op jit(solution)/shard_map/ppermute | solution.py:432
  20.1 8.2 %collective-permute-start.8 = (bf16[512,256]{1,0:T(8,128)(2,1)}, bf16[512,256]{1,0:T(8,128)(2,1)S(1)}, u32[]{:S(2)}, u32[]{:S(2)}) collective-permute-start(bf16[512,256]{1,0:T(8,128)(2,1)} %collective-permute-done.6.refs_1_), channel_id=1, source_target_pairs={{0,12},{4,0},{8,4},{12,8},{16,28},{20,16},{24,20},{28,24},{1,13},{... | collective-permute-start | bytes 786440 | tf_op jit(solution)/shard_map/ppermute | solution.py:434
  23.6 7.3 %collective-permute-start.10 = (bf16[512,256]{1,0:T(8,128)(2,1)S(1)}, bf16[512,256]{1,0:T(8,128)(2,1)S(1)}, u32[]{:S(2)}, u32[]{:S(2)}) collective-permute-start(bf16[512,256]{1,0:T(8,128)(2,1)S(1)} %collective-permute-done.9.refs_4_), channel_id=1, source_target_pairs={{0,16},{4,20},{8,24},{12,28},{16,0},{20,4},{24,8},{28,12},{1,17},{... | collective-permute-start | bytes 786440 | tf_op jit(solution)/shard_map/ppermute | solution.py:435
  25.5 30.2 %collective-permute-start.1 = (bf16[64,4096]{1,0:T(8,128)(2,1)}, bf16[64,4096]{1,0:T(8,128)(2,1)S(1)}, u32[]{:S(2)}, u32[]{:S(2)}) collective-permute-start(bf16[64,4096]{1,0:T(8,128)(2,1)} %get-tuple-element.63), channel_id=1, source_target_pairs={{0,1},{1,2},{2,3},{3,0},{4,5},{5,6},{6,7},{7,4},{8,9},{9,10},{10,1... | collective-permute-start | bytes 1572872 | tf_op jit(solution)/shard_map/ppermute | solution.py:425
  26.8 28.9 %collective-permute-start.2 = (bf16[64,4096]{1,0:T(8,128)(2,1)}, bf16[64,4096]{1,0:T(8,128)(2,1)S(1)}, u32[]{:S(2)}, u32[]{:S(2)}) collective-permute-start(bf16[64,4096]{1,0:T(8,128)(2,1)} %get-tuple-element.64), channel_id=1, source_target_pairs={{0,3},{1,0},{2,1},{3,2},{4,7},{5,4},{6,5},{7,6},{8,11},{9,8},{10,9... | collective-permute-start | bytes 1572872 | tf_op jit(solution)/shard_map/ppermute | solution.py:426
  28.2 6.9 %collective-permute-start.12 = (bf16[512,256]{1,0:T(8,128)(2,1)}, bf16[512,256]{1,0:T(8,128)(2,1)}, u32[]{:S(2)}, u32[]{:S(2)}) collective-permute-start(bf16[512,256]{1,0:T(8,128)(2,1)} %collective-permute-done.6.refs_1_), channel_id=1, source_target_pairs={{0,4},{4,8},{8,12},{12,0},{16,20},{20,24},{24,28},{28,16},{1,5},{5... | collective-permute-start | bytes 786440 | tf_op jit(solution)/shard_map/ppermute | solution.py:434
  29.0 26.8 %collective-permute-start.4 = (bf16[64,4096]{1,0:T(8,128)(2,1)S(1)}, bf16[64,4096]{1,0:T(8,128)(2,1)S(1)}, u32[]{:S(2)}, u32[]{:S(2)}) collective-permute-start(bf16[64,4096]{1,0:T(8,128)(2,1)S(1)} %collective-permute-done.refs_1_), channel_id=1, source_target_pairs={{0,1},{1,2},{2,3},{3,0},{4,5},{5,6},{6,7},{7,4},{8,9},{9,10},{10,1... | collective-permute-start | bytes 1572872 | tf_op jit(solution)/shard_map/ppermute | solution.py:423
  31.6 24.1 %collective-permute-start.5 = (bf16[64,4096]{1,0:T(8,128)(2,1)S(1)}, bf16[64,4096]{1,0:T(8,128)(2,1)S(1)}, u32[]{:S(2)}, u32[]{:S(2)}) collective-permute-start(bf16[64,4096]{1,0:T(8,128)(2,1)S(1)} %collective-permute-done.3.refs_4_), channel_id=1, source_target_pairs={{0,3},{1,0},{2,1},{3,2},{4,7},{5,4},{6,5},{7,6},{8,11},{9,8},{10,9... | collective-permute-start | bytes 1572872 | tf_op jit(solution)/shard_map/ppermute | solution.py:424
  35.2 125.7 %collective-permute-start.23 = (bf16[4096,256]{1,0:T(8,128)(2,1)}, bf16[4096,256]{1,0:T(8,128)(2,1)}, u32[]{:S(2)}, u32[]{:S(2)}) collective-permute-start(bf16[4096,256]{1,0:T(8,128)(2,1)} %pad_maximum_fusion), channel_id=1, source_target_pairs={{0,96},{32,0},{64,32},{96,64},{1,97},{33,1},{65,33},{97,65},{2,98}... | collective-permute-start | bytes 6291464 | tf_op jit(solution)/shard_map/ppermute | solution.py:442
  81.0 6.1 %collective-permute-start.26 = (bf16[2,128,128]{2,1,0:T(8,128)(2,1)S(1)}, bf16[2,128,128]{2,1,0:T(8,128)(2,1)S(1)}, u32[]{:S(2)}, u32[]{:S(2)}) collective-permute-start(bf16[2,128,128]{2,1,0:T(8,128)(2,1)S(1)} %get-tuple-element.57), channel_id=1, source_target_pairs={{0,12},{4,0},{8,4},{12,8},{16,28},{20,16},{24,20},{28,24},{1,13},{... | collective-permute-start | bytes 196616 | tf_op jit(solution)/shard_map/ppermute | solution.py:465
  81.4 6.8 %collective-permute-start.25 = (bf16[2,128,128]{2,1,0:T(8,128)(2,1)S(1)}, bf16[2,128,128]{2,1,0:T(8,128)(2,1)S(1)}, u32[]{:S(2)}, u32[]{:S(2)}) collective-permute-start(bf16[2,128,128]{2,1,0:T(8,128)(2,1)S(1)} %get-tuple-element.56), channel_id=1, source_target_pairs={{0,8},{4,12},{8,0},{12,4},{16,24},{20,28},{24,16},{28,20},{1,9},{5... | collective-permute-start | bytes 196616 | tf_op jit(solution)/shard_map/ppermute | solution.py:465
  85.0 24.6 %collective-permute-start.20 = (bf16[2,512,128]{2,1,0:T(8,128)(2,1)S(1)}, bf16[2,512,128]{2,1,0:T(8,128)(2,1)S(1)}, u32[]{:S(2)}, u32[]{:S(2)}) collective-permute-start(bf16[2,512,128]{2,1,0:T(8,128)(2,1)S(1)} %get-tuple-element.50), channel_id=1, source_target_pairs={{0,12},{4,0},{8,4},{12,8},{16,28},{20,16},{24,20},{28,24},{1,13},{... | collective-permute-start | bytes 786440 | tf_op jit(solution)/shard_map/ppermute | solution.py:465
  87.2 9.4 %collective-permute-start.16 = (bf16[2,384,128]{2,1,0:T(8,128)(2,1)S(1)}, bf16[2,384,128]{2,1,0:T(8,128)(2,1)S(1)}, u32[]{:S(2)}, u32[]{:S(2)}) collective-permute-start(bf16[2,384,128]{2,1,0:T(8,128)(2,1)S(1)} %get-tuple-element.46), channel_id=1, source_target_pairs={{0,12},{4,0},{8,4},{12,8},{16,28},{20,16},{24,20},{28,24},{1,13},{... | collective-permute-start | bytes 589832 | tf_op jit(solution)/shard_map/ppermute | solution.py:465
  88.3 10.9 %collective-permute-start.15 = (bf16[2,384,128]{2,1,0:T(8,128)(2,1)S(1)}, bf16[2,384,128]{2,1,0:T(8,128)(2,1)S(1)}, u32[]{:S(2)}, u32[]{:S(2)}) collective-permute-start(bf16[2,384,128]{2,1,0:T(8,128)(2,1)S(1)} %get-tuple-element.45), channel_id=1, source_target_pairs={{0,8},{4,12},{8,0},{12,4},{16,24},{20,28},{24,16},{28,20},{1,9},{5... | collective-permute-start | bytes 589832 | tf_op jit(solution)/shard_map/ppermute | solution.py:465
  92.7 10.1 %collective-permute-start.14 = (bf16[2,384,128]{2,1,0:T(8,128)(2,1)S(1)}, bf16[2,384,128]{2,1,0:T(8,128)(2,1)S(1)}, u32[]{:S(2)}, u32[]{:S(2)}) collective-permute-start(bf16[2,384,128]{2,1,0:T(8,128)(2,1)S(1)} %get-tuple-element.44), channel_id=1, source_target_pairs={{0,4},{4,8},{8,12},{12,0},{16,20},{20,24},{24,28},{28,16},{1,5},{5... | collective-permute-start | bytes 589832 | tf_op jit(solution)/shard_map/ppermute | solution.py:465
  96.6 13.1 %collective-permute-start.19 = (bf16[2,512,128]{2,1,0:T(8,128)(2,1)S(1)}, bf16[2,512,128]{2,1,0:T(8,128)(2,1)S(1)}, u32[]{:S(2)}, u32[]{:S(2)}) collective-permute-start(bf16[2,512,128]{2,1,0:T(8,128)(2,1)S(1)} %get-tuple-element.49), channel_id=1, source_target_pairs={{0,8},{4,12},{8,0},{12,4},{16,24},{20,28},{24,16},{28,20},{1,9},{5... | collective-permute-start | bytes 786440 | tf_op jit(solution)/shard_map/ppermute | solution.py:465
  99.2 10.5 %collective-permute-start.18 = (bf16[2,512,128]{2,1,0:T(8,128)(2,1)S(1)}, bf16[2,512,128]{2,1,0:T(8,128)(2,1)S(1)}, u32[]{:S(2)}, u32[]{:S(2)}) collective-permute-start(bf16[2,512,128]{2,1,0:T(8,128)(2,1)S(1)} %get-tuple-element.48), channel_id=1, source_target_pairs={{0,4},{4,8},{8,12},{12,0},{16,20},{20,24},{24,28},{28,16},{1,5},{5... | collective-permute-start | bytes 786440 | tf_op jit(solution)/shard_map/ppermute | solution.py:465
  102.8 55.0 %collective-permute-start.13 = (bf16[128,4096]{1,0:T(8,128)(2,1)S(1)}, bf16[128,4096]{1,0:T(8,128)(2,1)S(1)}, u32[]{:S(2)}, u32[]{:S(2)}) collective-permute-start(bf16[128,4096]{1,0:T(8,128)(2,1)S(1)} %convolution_convert_fusion.2), channel_id=1, source_target_pairs={{0,96},{32,0},{64,32},{96,64},{1,97},{33,1},{65,33},{97,65},{2,98}... | collective-permute-start | bytes 3145736 | tf_op jit(solution)/shard_map/ppermute | solution.py:493
  109.6 6.1 %collective-permute-start.17 = (bf16[384,128]{1,0:T(8,128)(2,1)S(1)}, bf16[384,128]{1,0:T(8,128)(2,1)S(1)}, u32[]{:S(2)}, u32[]{:S(2)}) collective-permute-start(bf16[384,128]{1,0:T(8,128)(2,1)S(1)} %fusion.29), channel_id=1, source_target_pairs={{0,16},{4,20},{8,24},{12,28},{16,0},{20,4},{24,8},{28,12},{1,17},{... | collective-permute-start | bytes 294920 | tf_op jit(solution)/shard_map/ppermute | solution.py:481
  109.9 9.4 %collective-permute-start.21 = (bf16[512,128]{1,0:T(8,128)(2,1)S(1)}, bf16[512,128]{1,0:T(8,128)(2,1)S(1)}, u32[]{:S(2)}, u32[]{:S(2)}) collective-permute-start(bf16[512,128]{1,0:T(8,128)(2,1)S(1)} %fusion.24), channel_id=1, source_target_pairs={{0,16},{4,20},{8,24},{12,28},{16,0},{20,4},{24,8},{28,12},{1,17},{... | collective-permute-start | bytes 393224 | tf_op jit(solution)/shard_map/ppermute | solution.py:481
  120.3 12.5 %collective-permute-start.28 = (bf16[64,4096]{1,0:T(8,128)(2,1)S(1)}, bf16[64,4096]{1,0:T(8,128)(2,1)S(1)}, u32[]{:S(2)}, u32[]{:S(2)}) collective-permute-start(bf16[64,4096]{1,0:T(8,128)(2,1)S(1)} %get-tuple-element.61), channel_id=1, source_target_pairs={{0,1},{1,2},{2,3},{3,0},{4,5},{5,6},{6,7},{7,4},{8,9},{9,10},{10,1... | collective-permute-start | bytes 1572872 | tf_op jit(solution)/shard_map/ppermute | solution.py:513
  122.4 40.9 %collective-permute-start.30 = (bf16[64,4096]{1,0:T(8,128)(2,1)S(1)}, bf16[64,4096]{1,0:T(8,128)(2,1)S(1)}, u32[]{:S(2)}, u32[]{:S(2)}) collective-permute-start(bf16[64,4096]{1,0:T(8,128)(2,1)S(1)} %slice.102), channel_id=1, source_target_pairs={{0,99},{1,96},{2,97},{3,98},{32,3},{33,0},{34,1},{35,2},{64,35},{6... | collective-permute-start | bytes 1572872 | tf_op jit(solution)/shard_map/ppermute | solution.py:518
  132.7 22.4 %collective-permute-start.22 = (bf16[128,256]{1,0:T(8,128)(2,1)S(1)}, bf16[128,256]{1,0:T(8,128)(2,1)S(1)}, u32[]{:S(2)}, u32[]{:S(2)}) collective-permute-start(bf16[128,256]{1,0:T(8,128)(2,1)S(1)} %pad_maximum_fusion.3), channel_id=1, source_target_pairs={{0,96},{32,0},{64,32},{96,64},{1,97},{33,1},{65,33},{97,65},{2,98}... | collective-permute-start | bytes 196616 | tf_op jit(solution)/shard_map/ppermute | solution.py:519
  132.8 22.2 %collective-permute-start.32 = (bf16[64,4096]{1,0:T(8,128)(2,1)S(1)}, bf16[64,4096]{1,0:T(8,128)(2,1)S(1)}, u32[]{:S(2)}, u32[]{:S(2)}) collective-permute-start(bf16[64,4096]{1,0:T(8,128)(2,1)S(1)} %get-tuple-element.62), channel_id=1, source_target_pairs={{0,3},{1,0},{2,1},{3,2},{4,7},{5,4},{6,5},{7,6},{8,11},{9,8},{10,9... | collective-permute-start | bytes 1572872 | tf_op jit(solution)/shard_map/ppermute | solution.py:514
  155.0 17.4 %collective-permute-start.31 = (bf16[64,4096]{1,0:T(8,128)(2,1)S(1)}, bf16[64,4096]{1,0:T(8,128)(2,1)S(1)}, u32[]{:S(2)}, u32[]{:S(2)}) collective-permute-start(bf16[64,4096]{1,0:T(8,128)(2,1)S(1)} %slice.104), channel_id=1, source_target_pairs={{0,97},{1,98},{2,99},{3,96},{32,1},{33,2},{34,3},{35,0},{64,33},{6... | collective-permute-start | bytes 1572872 | tf_op jit(solution)/shard_map/ppermute | solution.py:517
  155.1 22.8 %collective-permute-start.29 = (bf16[64,4096]{1,0:T(8,128)(2,1)S(1)}, bf16[64,4096]{1,0:T(8,128)(2,1)S(1)}, u32[]{:S(2)}, u32[]{:S(2)}) collective-permute-start(bf16[64,4096]{1,0:T(8,128)(2,1)S(1)} %add_convert_fusion.1), channel_id=1, source_target_pairs={{0,97},{1,98},{2,99},{3,96},{32,1},{33,2},{34,3},{35,0},{64,33},{6... | collective-permute-start | bytes 1572872 | tf_op jit(solution)/shard_map/ppermute | solution.py:522
  157.8 20.2 %collective-permute-start.33 = (bf16[64,4096]{1,0:T(8,128)(2,1)S(1)}, bf16[64,4096]{1,0:T(8,128)(2,1)S(1)}, u32[]{:S(2)}, u32[]{:S(2)}) collective-permute-start(bf16[64,4096]{1,0:T(8,128)(2,1)S(1)} %add_convert_fusion), channel_id=1, source_target_pairs={{0,99},{1,96},{2,97},{3,98},{32,3},{33,0},{34,1},{35,2},{64,35},{6... | collective-permute-start | bytes 1572872 | tf_op jit(solution)/shard_map/ppermute | solution.py:524
  (22 other events, 113.1 us)
